TPU v7x, 32 devices: a whole 2x2x4 slice. The times are simulated.
32 devices in a mesh: rep: 2 (over y), grp: 2 (over core), blk: 8 (over z, x).
Axes of the slice: x: 2, y: 2, z: 4, core: 2. Of those that a mesh axis runs over, the one named last changes fastest.
Arguments:
- queries: bfloat16 [2048, 8, 576], P(('rep', 'grp'), 'blk'), parts along dimension 0, may hold values from -64 to 64
- latents: bfloat16 [2048, 576], P(('rep', 'grp', 'blk')), parts along dimension 0, may hold values from -12 to 12
- out_grad: bfloat16 [2048, 8, 512], P(('rep', 'grp'), 'blk'), parts along dimension 0, may hold values from -6 to 6
- first_key: int32 [2048], P(('rep', 'grp')), parts along dimension 0, may hold values from 0 to 127, as said below
Outputs:
- query_grad: bfloat16 [2048, 8, 576], P(('rep', 'grp'), 'blk'), parts along dimension 0
- latent_grad: bfloat16 [2048, 576], P(('rep', 'grp', 'blk')), parts along dimension 0
There are 2 independent parts, one for each index of `rep`. A program takes and returns all parts, laid end to end along the dimension named above; each array names one. Nothing has to cross between parts.
Inputs may be any that keep to these rules, and one draw needn't show every extreme that they name: `first_key`: 0 for tokens of the first block; for a token of block b >= 1 a position among the first 128 of block b - 1.
All inputs are finite; a program needn't handle non-finite values.
Results may differ from a plain program's by a relative error of at most 0.0055.
Values may be sent and summed in bfloat16 or wider, within the bound.
No kernel may reach another device: no remote copies, remote signals or barrier semaphores. Data moves between devices by JAX's collectives and lax.ppermute only.
A program may use at most 64 MiB of HBM per device.

v0:
```python
import jax
import jax.numpy as jnp
from jax import lax
from jax.sharding import PartitionSpec as P

score_scale = 192.0 ** (-0.5)


def shifted(shard, axis, by):
    count = lax.axis_size(axis)
    pairs = [(i, i + by) for i in range(count) if 0 <= i + by < count]
    return lax.ppermute(shard, axis, pairs)


def attend_grads(query_blk, grad_blk, key_rows, visible):
    count, head_count, width = query_blk.shape
    query_rows = query_blk.reshape(count * head_count, width)
    grad_rows = grad_blk.reshape(count * head_count, -1)
    rank_width = grad_rows.shape[1]
    value_rows = key_rows[:, :rank_width]
    scores = jnp.dot(query_rows, key_rows.T, preferred_element_type=jnp.float32) * score_scale
    scores = scores.reshape(count, head_count, -1)
    mask_three = visible[:, None, :]
    row_max = jnp.max(jnp.where(mask_three, scores, -jnp.inf), axis=-1, keepdims=True)
    total = jnp.sum(jnp.where(mask_three, jnp.exp(scores - row_max), 0.0), axis=-1, keepdims=True)
    log_norm = row_max + jnp.log(total)
    attn_probs = jnp.where(mask_three, jnp.exp(scores - log_norm), 0.0).astype(jnp.bfloat16)
    attn_probs = attn_probs.reshape(count * head_count, -1)
    outputs = jnp.dot(attn_probs, value_rows, preferred_element_type=jnp.float32)
    row_delta = jnp.sum(grad_rows.astype(jnp.float32) * outputs, axis=-1, keepdims=True)
    prob_grad = jnp.dot(grad_rows, value_rows.T, preferred_element_type=jnp.float32)
    score_grad = (attn_probs.astype(jnp.float32) * (prob_grad - row_delta) * score_scale).astype(
        jnp.bfloat16
    )
    query_grad = jnp.dot(score_grad, key_rows, preferred_element_type=jnp.float32).astype(
        jnp.bfloat16
    )
    latent_part = jnp.dot(score_grad.T, query_rows, preferred_element_type=jnp.float32)
    value_part = jnp.dot(attn_probs.T, grad_rows, preferred_element_type=jnp.float32)
    latent_part = jnp.concatenate(
        [latent_part[:, :rank_width] + value_part, latent_part[:, rank_width:]], axis=1
    )
    return (query_grad.reshape(count, head_count, width), latent_part)


def shards(queries, latents, out_grad, first_key):
    block_len = queries.shape[0]
    head_local = queries.shape[1]
    width = queries.shape[2]
    rank_width = out_grad.shape[2]
    group_index = lax.axis_index("grp")
    own_block = lax.all_gather(latents, "blk", axis=0, tiled=True)
    prev_block = shifted(own_block, "grp", 1)
    key_rows = jnp.concatenate([prev_block, own_block], axis=0)
    key_iota = jnp.arange(2 * block_len, dtype=jnp.int32)
    key_pos = key_iota + (group_index - 1) * block_len
    in_prev = key_iota < block_len
    piece = min(512, block_len)
    pieces = block_len // piece
    query_steps = queries.reshape(pieces, piece, head_local, width)
    grad_steps = out_grad.reshape(pieces, piece, head_local, rank_width)
    first_steps = first_key.reshape(pieces, piece)
    pos_steps = (jnp.arange(block_len, dtype=jnp.int32) + group_index * block_len).reshape(
        pieces, piece
    )

    def scan_step(carry, items):
        query_blk, grad_blk, first_blk, pos_blk = items
        prev_ok = (key_pos[None, :] >= first_blk[:, None]) & (group_index > 0)
        own_ok = key_pos[None, :] <= pos_blk[:, None]
        visible = jnp.where(in_prev[None, :], prev_ok, own_ok)
        query_part, latent_part = attend_grads(query_blk, grad_blk, key_rows, visible)
        return (carry + latent_part, query_part)

    carry_init = jnp.zeros((2 * block_len, width), jnp.float32)
    latent_part, query_blocks = lax.scan(
        scan_step, carry_init, (query_steps, grad_steps, first_steps, pos_steps)
    )
    query_grad = query_blocks.reshape(block_len, head_local, width)
    prev_part = latent_part[:block_len]
    own_part = latent_part[block_len:]
    from_later = shifted(prev_part.astype(jnp.bfloat16), "grp", -1).astype(prev_part.dtype)
    latent_total = lax.psum_scatter(own_part + from_later, "blk", scatter_dimension=0, tiled=True)
    return (query_grad, latent_total.astype(jnp.bfloat16))


def solution(mesh):
    placed = (
        P(("rep", "grp"), "blk", None),
        P(("rep", "grp", "blk"), None),
        P(("rep", "grp"), "blk", None),
        P(("rep", "grp")),
    )
    return jax.shard_map(
        shards,
        mesh=mesh,
        in_specs=placed,
        out_specs=(P(("rep", "grp"), "blk", None), P(("rep", "grp", "blk"), None)),
        check_vma=False,
    )
```

profile of v0, /device:TPU:0, one launch (start us, length us, event | category | flops | bytes accessed | tf_op | source)
XLA Modules:
  0.0 132.1 jit_solution(18271201214269916155)
XLA Ops:
  7.2 0.0 copy-start
  7.2 0.0 copy-start.1
  7.2 0.0 copy-start.4
  7.2 0.0 reduce-scatter.4.cloned.1.call-start
  7.2 33.8 %all_gather.3 = bf16[512,576]{1,0:T(8,128)(2,1)S(1)} all-gather(bf16[64,576]{1,0:T(8,128)(2,1)} %param.5), channel_id=1, replica_groups=mesh['rep'=2,'grp'=2,'blk'=8] {'blk'}, dimensions={0}, use_global_device_ids=true | all-gather | bytes 663552 | tf_op jit(solution)/shard_map/all_gather | solution.py:52
  41.1 0.2 copy.11
  41.3 1.3 %collective-permute-start = (bf16[512,576]{0,1:T(8,128)(2,1)S(1)}, bf16[512,576]{0,1:T(8,128)(2,1)S(1)}, u32[]{:S(2)}, u32[]{:S(2)}) collective-permute-start(bf16[512,576]{0,1:T(8,128)(2,1)S(1)} %copy.11), channel_id=1, source_target_pairs={{0,8},{1,9},{2,10},{3,11},{4,12},{5,13},{6,14},{7,15},{16,24},{17,... | collective-permute-start | bytes 1769480 | tf_op jit(solution)/shard_map/ppermute | solution.py:12
  42.6 0.0 copy-done.1
  42.7 1.0 copy.13
  43.7 0.5 collective-permute-done
  44.2 0.3 copy.12
  44.5 0.0 copy-done
  44.5 1.4 %fusion.2 = (f32[512]{0:T(512)S(1)}, f32[1024,512]{1,0:T(8,128)S(1)}) fusion(s32[512]{0:T(512)S(1)} %iota_add_fusion.1, pred[]{:T(512)S(6)} %gt.4, s32[512]{0:T(512)S(1)} %copy-done.4, s32[1024]{0:T(1024)S(1)} %iota_add_fusion, pred[1024]{0:T(1024)(128)(4,1)S(1)} %iota_compare_fusion, bf16[512,1,576]{0,2,1:T(8,128)(2,1)S(1)} %copy-done, ...), kind=kOutput, calls=%fused_computation.9 | convolution fusion | flops 610008576 | bytes 3877889 | tf_op jit(solution)/shard_map/while/body/eval_jaxpr/dot_general | solution.py:21
  45.9 1.2 fusion.5
  47.1 0.0 copy-start.3
  47.2 1.2 fusion.8
  48.4 0.0 copy-done.3
  48.4 0.8 fusion.10
  49.2 0.0 copy-done.2
  49.2 0.8 fusion.1
  50.0 0.8 fusion.15
  50.8 0.8 slice_add_fusion
  51.6 0.1 fusion.13
  51.7 1.3 collective-permute-start.1
  53.0 2.6 %collective-permute-done.1 = bf16[512,576]{0,1:T(8,128)(2,1)S(1)} collective-permute-done((bf16[512,576]{0,1:T(8,128)(2,1)S(1)}, bf16[512,576]{0,1:T(8,128)(2,1)S(1)}, u32[]{:S(2)}, u32[]{:S(2)}) %collective-permute-start.1) | collective-permute-done | bytes 589856 | tf_op jit(solution)/shard_map/ppermute | solution.py:12
  55.6 0.2 fusion.12
  55.8 1.5 %copy.15 = f32[512,576]{1,0:T(8,128)} copy(f32[512,576]{0,1:T(8,128)S(1)} %fusion.12) | data formatting | bytes 2359296
  57.2 0.0 reduce-scatter.4.cloned.1.call-update
  57.3 2.7 %fusion.9 = bf16[512,1,576]{0,2,1:T(8,128)(2,1)} fusion(bf16[512,1024]{0,1:T(8,128)(2,1)S(1)} %fusion.1, bf16[512,576]{1,0:T(8,128)(2,1)S(1)} %all_gather.3, bf16[512,576]{1,0:T(8,128)(2,1)} %copy-done.2), kind=kOutput, calls=%fused_computation.20 | convolution fusion | flops 606633984 | bytes 2818048 | tf_op jit(solution)/shard_map/while/body/eval_jaxpr/dot_general | solution.py:35
  60.0 63.4 %reduce-scatter.4.cloned.1.call-done = f32[64,576]{1,0:T(8,128)} async-done(((f32[512,576]{1,0:T(8,128)}), f32[64,576]{1,0:T(8,128)}) %reduce-scatter.4.cloned.1.call-update) | async-done | bytes 147472
  123.4 1.0 copy.16
  124.5 0.8 copy.14
  (7 shorter events, 0.0 us)
Async XLA Ops:
  7.2 37.4 %copy-start = (bf16[512,1,576]{0,2,1:T(8,128)(2,1)S(1)}, bf16[512,1,576]{0,2,1:T(8,128)(2,1)}, u32[]{:S(2)}) copy-start(bf16[512,1,576]{0,2,1:T(8,128)(2,1)} %param.4) | copy-start | bytes 1769476
  7.2 35.5 %copy-start.1 = (bf16[512,1,512]{2,0,1:T(8,128)(2,1)S(1)}, bf16[512,1,512]{2,0,1:T(8,128)(2,1)}, u32[]{:S(2)}) copy-start(bf16[512,1,512]{2,0,1:T(8,128)(2,1)} %param.6) | copy-start | bytes 1572868
  7.2 37.3 %copy-start.4 = (s32[512]{0:T(512)S(1)}, s32[512]{0:T(512)}, u32[]{:S(2)}) copy-start(s32[512]{0:T(512)} %param.7) | copy-start | bytes 6148
  7.2 116.2 %reduce-scatter.4.cloned.1.call-start = ((), (), s32[]{:S(2)}) async-start(), calls=%async_computation.1 | async-start | bytes 1474560
  41.3 2.9 %collective-permute-start = (bf16[512,576]{0,1:T(8,128)(2,1)S(1)}, bf16[512,576]{0,1:T(8,128)(2,1)S(1)}, u32[]{:S(2)}, u32[]{:S(2)}) collective-permute-start(bf16[512,576]{0,1:T(8,128)(2,1)S(1)} %copy.11), channel_id=1, source_target_pairs={{0,8},{1,9},{2,10},{3,11},{4,12},{5,13},{6,14},{7,15},{16,24},{17,... | collective-permute-start | bytes 1769480 | tf_op jit(solution)/shard_map/ppermute | solution.py:12
  44.5 4.6 %copy-start.2 = (bf16[512,576]{1,0:T(8,128)(2,1)}, bf16[512,576]{1,0:T(8,128)(2,1)S(1)}, u32[]{:S(2)}) copy-start(bf16[512,576]{1,0:T(8,128)(2,1)S(1)} %copy.12) | copy-start | bytes 1769476
  47.1 1.2 copy-start.3
  51.7 3.9 %collective-permute-start.1 = (bf16[512,576]{0,1:T(8,128)(2,1)S(1)}, bf16[512,576]{0,1:T(8,128)(2,1)S(1)}, u32[]{:S(2)}, u32[]{:S(2)}) collective-permute-start(bf16[512,576]{0,1:T(8,128)(2,1)S(1)} %fusion.13), channel_id=1, source_target_pairs={{8,0},{9,1},{10,2},{11,3},{12,4},{13,5},{14,6},{15,7},{24,16},{25,... | collective-permute-start | bytes 1769480 | tf_op jit(solution)/shard_map/ppermute | solution.py:12
Sparse Core Ops, SparseCore 0:
  57.4 65.9 reduce-scatter.3
where the time goes:
time: 132 us
  waiting for transfers between devices  66.6 us (50%)
  blocking collectives  33.8 us (26%)
  between operations  14.2 us (11%)
  matrix products  7.27 us (6%)
  local copies, waits for them, and re-layouts  4.87 us (4%)
  other arithmetic  2.68 us (2%)
  starting transfers between devices  2.66 us (2%)
    unnamed x2, waiting for transfers between devices  63.4 us
    all_gather x1, blocking collectives, shards(): own_block = lax.all_gather(latents, 'blk', axis=0, tiled=True)  33.8 us
    unnamed x14, local copies, waits for them, and re-layouts  4.32 us
    ppermute x2, waiting for transfers between devices, shifted(): return lax.ppermute(shard, axis, pairs)  3.14 us
    dot_general x1, matrix products, attend_grads(): jnp.dot(score_grad, key_rows, preferred_element_type=jnp.float32)  2.73 us
  transfers between devices with their start and end apart: 3, of which 3 were waited for; matrix products, arithmetic and copies ran while one was open for 3% of the time, Pallas kernels for 0%

commit v1 on v0

v1 whole, which is shorter than its diff:
```python
import functools

import jax
import jax.numpy as jnp
from jax import lax
from jax.experimental import pallas as pl
from jax.experimental.pallas import tpu as pltpu
from jax.sharding import PartitionSpec as P

score_scale = 192.0 ** (-0.5)
masked_score = -1e30
f32 = jnp.float32
bf16 = jnp.bfloat16


def dot_nn(a, b):
    return lax.dot_general(a, b, (((1,), (0,)), ((), ())), preferred_element_type=f32)


def dot_nt(a, b):
    return lax.dot_general(a, b, (((1,), (1,)), ((), ())), preferred_element_type=f32)


def dot_tn(a, b):
    return lax.dot_general(a, b, (((0,), (0,)), ((), ())), preferred_element_type=f32)


def attend_kernel(pieces, scalars, first_ref, query_ref, grad_ref, *refs):
    own_refs, prev_refs = refs[:pieces], refs[pieces : 2 * pieces]
    prev_out, own_out, score_grad_out, keys_out = refs[2 * pieces : 2 * pieces + 4]
    score_scr, prob_grad_scr, probs_scr = refs[2 * pieces + 4 :]
    block_len = grad_ref.shape[0]
    rank_width = grad_ref.shape[1]
    piece_len = block_len // pieces
    tile = min(256, block_len)
    tiles = block_len // tile
    blk_index = scalars[0]
    group_index = scalars[1]

    for part, piece_refs in ((0, prev_refs), (1, own_refs)):
        for m in range(pieces):
            start = part * block_len + m * piece_len
            keys_out[start : start + piece_len, :] = piece_refs[m][...]

    token_pos = lax.broadcasted_iota(jnp.int32, (1, block_len), 1)

    def visible(c):
        row = lax.broadcasted_iota(jnp.int32, (tile, 1), 0) + (c % tiles) * tile
        key_pos = (blk_index ^ (row // piece_len)) * piece_len + row % piece_len
        if c < tiles:
            return key_pos + (group_index - 1) * block_len >= first_ref[...]
        return key_pos <= token_pos

    def run(chunks):
        rows = {c: pl.ds(c * tile, tile) for c in chunks}
        peak = None
        for c in chunks:
            keys = keys_out[rows[c], :]
            scores = dot_nn(keys, query_ref[...]) * score_scale
            scores = jnp.where(visible(c), scores, masked_score)
            score_scr[rows[c], :] = scores
            top = jnp.max(scores, axis=0, keepdims=True)
            peak = top if peak is None else jnp.maximum(peak, top)
            prob_grad_scr[rows[c], :] = dot_nt(keys[:, :rank_width], grad_ref[...])
        total = 0.0
        for c in chunks:
            lifted = jnp.exp(score_scr[rows[c], :] - peak)
            score_scr[rows[c], :] = lifted
            total = total + jnp.sum(lifted, axis=0, keepdims=True)
        inverse = 1.0 / total
        delta = 0.0
        for c in chunks:
            probs = (score_scr[rows[c], :] * inverse).astype(bf16)
            probs_scr[rows[c], :] = probs
            delta = delta + jnp.sum(
                probs.astype(f32) * prob_grad_scr[rows[c], :], axis=0, keepdims=True
            )
        for c in chunks:
            probs = probs_scr[rows[c], :]
            score_grad = (
                probs.astype(f32) * (prob_grad_scr[rows[c], :] - delta) * score_scale
            ).astype(bf16)
            score_grad_out[rows[c], :] = score_grad
            latent_part = dot_nt(score_grad, query_ref[...])
            value_part = dot_nn(probs, grad_ref[...])
            target = prev_out if c < tiles else own_out
            out_rows = pl.ds((c % tiles) * tile, tile)
            target[out_rows, :rank_width] = (latent_part[:, :rank_width] + value_part).astype(
                target.dtype
            )
            target[out_rows, rank_width:] = latent_part[:, rank_width:].astype(target.dtype)

    @pl.when(group_index > 0)
    def _():
        run(range(2 * tiles))

    @pl.when(group_index == 0)
    def _():
        run(range(tiles, 2 * tiles))
        score_grad_out[:block_len, :] = jnp.zeros((block_len, block_len), bf16)
        prev_out[...] = jnp.zeros(prev_out.shape, prev_out.dtype)


def query_grad_kernel(keys_ref, score_grad_ref, out_ref):
    out_ref[...] = dot_tn(keys_ref[...], score_grad_ref[...]).astype(bf16)


def vmem():
    return pl.BlockSpec(memory_space=pltpu.VMEM)


def attend(scalars, first_row, query_t, grad_rows, own, prev):
    pieces = len(own)
    block_len = grad_rows.shape[0]
    width = query_t.shape[0]
    keys = (2 * block_len, width)
    pairs = (2 * block_len, block_len)
    return pl.pallas_call(
        functools.partial(attend_kernel, pieces),
        out_shape=(
            jax.ShapeDtypeStruct((block_len, width), bf16),
            jax.ShapeDtypeStruct((block_len, width), f32),
            jax.ShapeDtypeStruct(pairs, bf16),
            jax.ShapeDtypeStruct(keys, bf16),
        ),
        in_specs=[pl.BlockSpec(memory_space=pltpu.SMEM)] + [vmem()] * (3 + 2 * pieces),
        out_specs=(vmem(),) * 4,
        scratch_shapes=[pltpu.VMEM(pairs, f32), pltpu.VMEM(pairs, f32), pltpu.VMEM(pairs, bf16)],
        name="attend",
    )(scalars, first_row, query_t, grad_rows, *own, *prev)


def query_grads(keys, score_grad):
    return pl.pallas_call(
        query_grad_kernel,
        out_shape=jax.ShapeDtypeStruct((keys.shape[1], score_grad.shape[1]), bf16),
        in_specs=[vmem(), vmem()],
        out_specs=vmem(),
        name="query_grad",
    )(keys, score_grad)


def shifted(shard, axis, by):
    count = lax.axis_size(axis)
    pairs = [(i, i + by) for i in range(count) if 0 <= i + by < count]
    return lax.ppermute(shard, axis, pairs)


def swapped(shard, mask):
    count = lax.axis_size("blk")
    return lax.ppermute(shard, "blk", [(i, i ^ mask) for i in range(count)])


def gather_pieces(latents, count):
    pieces = [latents] + [None] * (count - 1)
    for m in range(2, count, 2):
        pieces[m] = swapped(latents, m)
    pieces[1] = swapped(latents, 1)
    for m in range(2, count, 2):
        pieces[m + 1] = swapped(pieces[m], 1)
    return pieces


def scatter_pieces(parts, count):
    far = {}
    for m in range(count - 2, -1, -2):
        far[m] = swapped(parts[m + 1].astype(bf16), 1)
    sums = {m: parts[m] + far[m].astype(f32) for m in far}
    total = sums[0]
    for m in range(count - 2, 0, -2):
        total = total + swapped(sums[m].astype(bf16), m).astype(f32)
    return total


def shards(queries, latents, out_grad, first_key):
    block_len, head_local, width = queries.shape
    rank_width = out_grad.shape[2]
    count = lax.axis_size("blk")
    by_swaps = count in (2, 4, 8, 16)
    group_index = lax.axis_index("grp")
    blk_index = lax.axis_index("blk")
    if by_swaps:
        own = gather_pieces(latents, count)
    else:
        own = [lax.all_gather(latents, "blk", axis=0, tiled=True)]
        blk_index = jnp.zeros_like(blk_index)
    prev = [shifted(piece, "grp", 1) for piece in own]
    scalars = jnp.stack([blk_index, group_index]).astype(jnp.int32)
    first_row = first_key.reshape(1, block_len)
    query_parts = []
    own_part = prev_part = None
    for h in range(head_local):
        prev_h, own_h, score_grad, keys = attend(
            scalars, first_row, queries[:, h, :].T, out_grad[:, h, :], own, prev
        )
        query_parts.append((keys, score_grad))
        own_part = own_h if h == 0 else own_part + own_h
        prev_part = prev_h if h == 0 else prev_part.astype(f32) + prev_h.astype(f32)
    from_later = shifted(prev_part.astype(bf16), "grp", -1)
    if by_swaps:
        piece_len = block_len // count
        parts = []
        for m in range(count):
            rows = slice(m * piece_len, (m + 1) * piece_len)
            parts.append(own_part[rows] + from_later[rows].astype(f32))
        latent_total = scatter_pieces(parts, count)
    else:
        latent_total = lax.psum_scatter(
            own_part + from_later.astype(f32), "blk", scatter_dimension=0, tiled=True
        )
    query_grad = jnp.stack([query_grads(k, s).T for k, s in query_parts], axis=1)
    return (query_grad, latent_total.astype(bf16))


def solution(mesh):
    placed = (
        P(("rep", "grp"), "blk", None),
        P(("rep", "grp", "blk"), None),
        P(("rep", "grp"), "blk", None),
        P(("rep", "grp")),
    )
    return jax.shard_map(
        shards,
        mesh=mesh,
        in_specs=placed,
        out_specs=(P(("rep", "grp"), "blk", None), P(("rep", "grp", "blk"), None)),
        check_vma=False,
    )
```

time: 132 us -> 57.9 us (0.44)
  waiting for transfers between devices: 66.6 us -> 11.3 us
  blocking collectives: 33.8 us -> 0 us
  starting transfers between devices: 2.66 us -> 31.4 us
  between operations: 14.2 us -> 0.98 us
  Pallas kernels: 0 us -> 9.06 us
  matrix products: 7.27 us -> 0 us
  local copies, waits for them, and re-layouts: 4.87 us -> 3.33 us
    unnamed x2 -> x0, waiting for transfers between devices: 63.4 us -> none
    all_gather x1 -> x0, blocking collectives: 33.8 us -> none  [shards(): own_block = lax.all_gather(latents, 'blk', axis=0, tiled=True)]
    ppermute x0 -> x14, starting transfers between devices: none -> 19.6 us  [swapped(): return lax.ppermute(shard, 'blk', [(i, i ^ mask) for i in range(count)])]
    ppermute x2 -> x9, starting transfers between devices: 2.62 us -> 11.7 us  [shifted(): return lax.ppermute(shard, axis, pairs)]
    pallas_call x0 -> x2, Pallas kernels: none -> 9.06 us  [the longest x1 5.82 us: attend(): pl.pallas_call(functools.partial(attend_kernel, pieces), out_shape=(jax.S...]
    ppermute x0 -> x14, waiting for transfers between devices: none -> 7.29 us  [swapped(): return lax.ppermute(shard, 'blk', [(i, i ^ mask) for i in range(count)])]
    dot_general x6 -> x0, matrix products: 7.27 us -> none  [the longest x1 2.73 us: attend_grads(): jnp.dot(score_grad, key_rows, preferred_element_type=jnp.float32)]
    unnamed x14 -> x40, local copies, waits for them, and re-layouts: 4.32 us -> 1.74 us
  transfers between devices with their start and end apart: 3 -> 23, of which waited for: 3 -> 7; matrix products, arithmetic and copies ran while one was open for 3% -> 2% of each run, Pallas kernels for 0% -> 6%
where the time goes in v1:
time: 57.9 us; the launch traced here: 57.5 us
  starting transfers between devices  31.4 us (54%)
  waiting for transfers between devices  11.3 us (20%)
  Pallas kernels  9.06 us (16%)
  local copies, waits for them, and re-layouts  3.33 us (6%)
  other arithmetic  1.44 us (2%)
  between operations  0.98 us (2%)
    ppermute x14, starting transfers between devices, swapped(): return lax.ppermute(shard, 'blk', [(i, i ^ mask) for i in range(count)])  19.6 us
    ppermute x9, starting transfers between devices, shifted(): return lax.ppermute(shard, axis, pairs)  11.7 us
    ppermute x14, waiting for transfers between devices, swapped(): return lax.ppermute(shard, 'blk', [(i, i ^ mask) for i in range(count)])  7.29 us
    pallas_call x1, Pallas kernels, attend(): pl.pallas_call(functools.partial(attend_kernel, pieces), out_shape=(jax.S...  5.82 us
    ppermute x9, waiting for transfers between devices, shifted(): return lax.ppermute(shard, axis, pairs)  4.05 us
    pallas_call x1, Pallas kernels, query_grads(): pl.pallas_call(query_grad_kernel, out_shape=jax.ShapeDtypeStruct((keys.sh...  3.24 us
    unnamed x40, local copies, waits for them, and re-layouts  1.74 us
    pallas_call x1, local copies, waits for them, and re-layouts, attend(): pl.pallas_call(functools.partial(attend_kernel, pieces), out_shape=(jax.S...  1.31 us
  transfers between devices with their start and end apart: 23, of which 7 were waited for; matrix products, arithmetic and copies ran while one was open for 2% of the time, Pallas kernels for 6%

profile of v1, /device:TPU:0, one launch (start us, length us, event | category | flops | bytes accessed | tf_op | source)
XLA Modules:
  0.0 57.5 jit_solution(14936819516217365013)
XLA Ops:
  0.6 5.1 %collective-permute-start.5 = (bf16[64,576]{1,0:T(8,128)(2,1)}, bf16[64,576]{1,0:T(8,128)(2,1)S(1)}, u32[]{:S(2)}, u32[]{:S(2)}) collective-permute-start(bf16[64,576]{1,0:T(8,128)(2,1)} %refs_0_.1), channel_id=1, source_target_pairs={{0,6},{1,7},{2,4},{3,5},{4,2},{5,3},{6,0},{7,1},{8,14},{9,15},{10,... | collective-permute-start | bytes 221192 | tf_op jit(solution)/shard_map/ppermute | solution.py:151
  5.8 0.6 %collective-permute-start.1 = (bf16[64,576]{1,0:T(8,128)(2,1)}, bf16[64,576]{1,0:T(8,128)(2,1)S(1)}, u32[]{:S(2)}, u32[]{:S(2)}) collective-permute-start(bf16[64,576]{1,0:T(8,128)(2,1)} %refs_0_.1), channel_id=1, source_target_pairs={{0,2},{1,3},{2,0},{3,1},{4,6},{5,7},{6,4},{7,5},{8,10},{9,11},{10,... | collective-permute-start | bytes 221192 | tf_op jit(solution)/shard_map/ppermute | solution.py:151
  6.4 1.6 %collective-permute-start = (bf16[64,576]{1,0:T(8,128)(2,1)}, bf16[64,576]{1,0:T(8,128)(2,1)S(1)}, u32[]{:S(2)}, u32[]{:S(2)}) collective-permute-start(bf16[64,576]{1,0:T(8,128)(2,1)} %refs_0_.1), channel_id=1, source_target_pairs={{0,1},{1,0},{2,3},{3,2},{4,5},{5,4},{6,7},{7,6},{8,9},{9,8},{10,11... | collective-permute-start | bytes 221192 | tf_op jit(solution)/shard_map/ppermute | solution.py:151
  8.1 1.3 %collective-permute-start.7 = (bf16[64,576]{1,0:T(8,128)(2,1)}, bf16[64,576]{1,0:T(8,128)(2,1)S(1)}, u32[]{:S(2)}, u32[]{:S(2)}) collective-permute-start(bf16[64,576]{1,0:T(8,128)(2,1)} %refs_0_.1), channel_id=1, source_target_pairs={{0,8},{1,9},{2,10},{3,11},{4,12},{5,13},{6,14},{7,15},{16,24},{17,... | collective-permute-start | bytes 221192 | tf_op jit(solution)/shard_map/ppermute | solution.py:146
  9.4 1.3 %collective-permute-start.13 = (bf16[64,576]{1,0:T(8,128)(2,1)S(1)}, bf16[64,576]{1,0:T(8,128)(2,1)S(1)}, u32[]{:S(2)}, u32[]{:S(2)}) collective-permute-start(bf16[64,576]{1,0:T(8,128)(2,1)S(1)} %collective-permute-done.5.refs_6_), channel_id=1, source_target_pairs={{0,8},{1,9},{2,10},{3,11},{4,12},{5,13},{6,14},{7,15},{16,24},{17,... | collective-permute-start | bytes 221192 | tf_op jit(solution)/shard_map/ppermute | solution.py:146
  10.7 2.2 %collective-permute-done.3.refs_4_ = bf16[64,576]{1,0:T(8,128)(2,1)S(1)} collective-permute-done((bf16[64,576]{1,0:T(8,128)(2,1)}, bf16[64,576]{1,0:T(8,128)(2,1)S(1)}, u32[]{:S(2)}, u32[]{:S(2)}) %collective-permute-start.3) | collective-permute-done | bytes 73760 | tf_op jit(solution)/shard_map/ppermute | solution.py:151
  12.8 1.5 %collective-permute-start.6 = (bf16[64,576]{1,0:T(8,128)(2,1)S(1)}, bf16[64,576]{1,0:T(8,128)(2,1)S(1)}, u32[]{:S(2)}, u32[]{:S(2)}) collective-permute-start(bf16[64,576]{1,0:T(8,128)(2,1)S(1)} %collective-permute-done.5.refs_6_), channel_id=1, source_target_pairs={{0,1},{1,0},{2,3},{3,2},{4,5},{5,4},{6,7},{7,6},{8,9},{9,8},{10,11... | collective-permute-start | bytes 221192 | tf_op jit(solution)/shard_map/ppermute | solution.py:151
  14.3 1.3 %collective-permute-start.11 = (bf16[64,576]{1,0:T(8,128)(2,1)S(1)}, bf16[64,576]{1,0:T(8,128)(2,1)S(1)}, u32[]{:S(2)}, u32[]{:S(2)}) collective-permute-start(bf16[64,576]{1,0:T(8,128)(2,1)S(1)} %collective-permute-done.3.refs_4_), channel_id=1, source_target_pairs={{0,8},{1,9},{2,10},{3,11},{4,12},{5,13},{6,14},{7,15},{16,24},{17,... | collective-permute-start | bytes 221192 | tf_op jit(solution)/shard_map/ppermute | solution.py:146
  15.7 0.6 %collective-permute-start.4 = (bf16[64,576]{1,0:T(8,128)(2,1)S(1)}, bf16[64,576]{1,0:T(8,128)(2,1)S(1)}, u32[]{:S(2)}, u32[]{:S(2)}) collective-permute-start(bf16[64,576]{1,0:T(8,128)(2,1)S(1)} %collective-permute-done.3.refs_4_), channel_id=1, source_target_pairs={{0,1},{1,0},{2,3},{3,2},{4,5},{5,4},{6,7},{7,6},{8,9},{9,8},{10,11... | collective-permute-start | bytes 221192 | tf_op jit(solution)/shard_map/ppermute | solution.py:151
  16.3 1.5 %collective-permute-start.2 = (bf16[64,576]{1,0:T(8,128)(2,1)S(1)}, bf16[64,576]{1,0:T(8,128)(2,1)S(1)}, u32[]{:S(2)}, u32[]{:S(2)}) collective-permute-start(bf16[64,576]{1,0:T(8,128)(2,1)S(1)} %collective-permute-done.1.refs_2_), channel_id=1, source_target_pairs={{0,1},{1,0},{2,3},{3,2},{4,5},{5,4},{6,7},{7,6},{8,9},{9,8},{10,11... | collective-permute-start | bytes 221192 | tf_op jit(solution)/shard_map/ppermute | solution.py:151
  17.8 1.3 %collective-permute-start.9 = (bf16[64,576]{1,0:T(8,128)(2,1)S(1)}, bf16[64,576]{1,0:T(8,128)(2,1)S(1)}, u32[]{:S(2)}, u32[]{:S(2)}) collective-permute-start(bf16[64,576]{1,0:T(8,128)(2,1)S(1)} %collective-permute-done.1.refs_2_), channel_id=1, source_target_pairs={{0,8},{1,9},{2,10},{3,11},{4,12},{5,13},{6,14},{7,15},{16,24},{17,... | collective-permute-start | bytes 221192 | tf_op jit(solution)/shard_map/ppermute | solution.py:146
  19.1 1.3 %collective-permute-start.8 = (bf16[64,576]{1,0:T(8,128)(2,1)S(1)}, bf16[64,576]{1,0:T(8,128)(2,1)S(1)}, u32[]{:S(2)}, u32[]{:S(2)}) collective-permute-start(bf16[64,576]{1,0:T(8,128)(2,1)S(1)} %collective-permute-done.refs_1_), channel_id=1, source_target_pairs={{0,8},{1,9},{2,10},{3,11},{4,12},{5,13},{6,14},{7,15},{16,24},{17,... | collective-permute-start | bytes 221192 | tf_op jit(solution)/shard_map/ppermute | solution.py:146
  20.4 1.3 %collective-permute-start.14 = (bf16[64,576]{1,0:T(8,128)(2,1)S(1)}, bf16[64,576]{1,0:T(8,128)(2,1)S(1)}, u32[]{:S(2)}, u32[]{:S(2)}) collective-permute-start(bf16[64,576]{1,0:T(8,128)(2,1)S(1)} %collective-permute-done.6.refs_7_), channel_id=1, source_target_pairs={{0,8},{1,9},{2,10},{3,11},{4,12},{5,13},{6,14},{7,15},{16,24},{17,... | collective-permute-start | bytes 221192 | tf_op jit(solution)/shard_map/ppermute | solution.py:146
  21.7 1.3 %collective-permute-start.12 = (bf16[64,576]{1,0:T(8,128)(2,1)S(1)}, bf16[64,576]{1,0:T(8,128)(2,1)S(1)}, u32[]{:S(2)}, u32[]{:S(2)}) collective-permute-start(bf16[64,576]{1,0:T(8,128)(2,1)S(1)} %collective-permute-done.4.refs_5_), channel_id=1, source_target_pairs={{0,8},{1,9},{2,10},{3,11},{4,12},{5,13},{6,14},{7,15},{16,24},{17,... | collective-permute-start | bytes 221192 | tf_op jit(solution)/shard_map/ppermute | solution.py:146
  23.0 1.3 %collective-permute-start.10 = (bf16[64,576]{1,0:T(8,128)(2,1)S(1)}, bf16[64,576]{1,0:T(8,128)(2,1)S(1)}, u32[]{:S(2)}, u32[]{:S(2)}) collective-permute-start(bf16[64,576]{1,0:T(8,128)(2,1)S(1)} %collective-permute-done.2.refs_3_), channel_id=1, source_target_pairs={{0,8},{1,9},{2,10},{3,11},{4,12},{5,13},{6,14},{7,15},{16,24},{17,... | collective-permute-start | bytes 221192 | tf_op jit(solution)/shard_map/ppermute | solution.py:146
  24.3 0.6 %pad_add_fusion.scalars = s32[2]{0:T(128)} fusion(s32[1]{0:T(128)} %bitcast.1, s32[1]{0:T(128)} %bitcast), kind=kLoop, calls=%fused_computation.8 | loop fusion | flops 2 | bytes 16 | tf_op jit(solution)/shard_map/stack | solution.py:188
  25.9 5.8 %attend.1 = (bf16[512,576]{1,0:T(8,128)(2,1)}, f32[512,576]{1,0:T(8,128)}, bf16[1024,512]{1,0:T(8,128)(2,1)}, bf16[1024,576]{1,0:T(8,128)(2,1)}) custom-call(s32[2]{0:T(128)} %pad_add_fusion.scalars, s32[1,512]{1,0:T(1,128)} %bitcast.13, bf16[576,512]{1,0:T(8,128)(2,1)} %bitcast.10, bf16[512,512]{1,0:T(8,128)(2,1)} %bitcast.12, bf16[64,576]{1,0:T(8,128)(2,1)} %refs_0_.1, ...), custom_call_target="tpu_custom_call" | custom-call | tf_op jit(solution)/shard_map/attend/pallas_call | solution.py:118
  31.7 1.3 %copy.6 = bf16[512,576]{0,1:T(8,128)(2,1)S(1)} copy(bf16[512,576]{1,0:T(8,128)(2,1)} %get-tuple-element.9) | data formatting | bytes 1179648 | tf_op jit(solution)/shard_map/attend/pallas_call | solution.py:118
  33.0 1.4 %collective-permute-start.15 = (bf16[512,576]{0,1:T(8,128)(2,1)S(1)}, bf16[512,576]{0,1:T(8,128)(2,1)S(1)}, u32[]{:S(2)}, u32[]{:S(2)}) collective-permute-start(bf16[512,576]{0,1:T(8,128)(2,1)S(1)} %copy.6), channel_id=1, source_target_pairs={{8,0},{9,1},{10,2},{11,3},{12,4},{13,5},{14,6},{15,7},{24,16},{25,... | collective-permute-start | bytes 1769480 | tf_op jit(solution)/shard_map/ppermute | solution.py:146
  34.5 3.8 %collective-permute-done.15 = bf16[512,576]{0,1:T(8,128)(2,1)S(1)} collective-permute-done((bf16[512,576]{0,1:T(8,128)(2,1)S(1)}, bf16[512,576]{0,1:T(8,128)(2,1)S(1)}, u32[]{:S(2)}, u32[]{:S(2)}) %collective-permute-start.15) | collective-permute-done | bytes 589856 | tf_op jit(solution)/shard_map/ppermute | solution.py:146
  39.2 0.6 %collective-permute-start.21 = (bf16[64,576]{1,0:T(8,128)(2,1)S(1)}, bf16[64,576]{1,0:T(8,128)(2,1)S(1)}, u32[]{:S(2)}, u32[]{:S(2)}) collective-permute-start(bf16[64,576]{1,0:T(8,128)(2,1)S(1)} %get-tuple-element.11), channel_id=1, source_target_pairs={{0,1},{1,0},{2,3},{3,2},{4,5},{5,4},{6,7},{7,6},{8,9},{9,8},{10,11... | collective-permute-start | bytes 221192 | tf_op jit(solution)/shard_map/ppermute | solution.py:151
  39.8 1.5 %collective-permute-start.19 = (bf16[64,576]{1,0:T(8,128)(2,1)S(1)}, bf16[64,576]{1,0:T(8,128)(2,1)S(1)}, u32[]{:S(2)}, u32[]{:S(2)}) collective-permute-start(bf16[64,576]{1,0:T(8,128)(2,1)S(1)} %get-tuple-element.12), channel_id=1, source_target_pairs={{0,1},{1,0},{2,3},{3,2},{4,5},{5,4},{6,7},{7,6},{8,9},{9,8},{10,11... | collective-permute-start | bytes 221192 | tf_op jit(solution)/shard_map/ppermute | solution.py:151
  41.3 0.6 collective-permute-start.17
  42.3 1.5 %collective-permute-start.16 = (bf16[64,576]{1,0:T(8,128)(2,1)S(1)}, bf16[64,576]{1,0:T(8,128)(2,1)S(1)}, u32[]{:S(2)}, u32[]{:S(2)}) collective-permute-start(bf16[64,576]{1,0:T(8,128)(2,1)S(1)} %get-tuple-element.10), channel_id=1, source_target_pairs={{0,1},{1,0},{2,3},{3,2},{4,5},{5,4},{6,7},{7,6},{8,9},{9,8},{10,11... | collective-permute-start | bytes 221192 | tf_op jit(solution)/shard_map/ppermute | solution.py:151
  43.8 0.8 %collective-permute-done.21 = bf16[64,576]{1,0:T(8,128)(2,1)S(1)} collective-permute-done((bf16[64,576]{1,0:T(8,128)(2,1)S(1)}, bf16[64,576]{1,0:T(8,128)(2,1)S(1)}, u32[]{:S(2)}, u32[]{:S(2)}) %collective-permute-start.21) | collective-permute-done | bytes 73760 | tf_op jit(solution)/shard_map/ppermute | solution.py:151
  44.6 1.8 %collective-permute-done.19 = bf16[64,576]{1,0:T(8,128)(2,1)S(1)} collective-permute-done((bf16[64,576]{1,0:T(8,128)(2,1)S(1)}, bf16[64,576]{1,0:T(8,128)(2,1)S(1)}, u32[]{:S(2)}, u32[]{:S(2)}) %collective-permute-start.19) | collective-permute-done | bytes 73760 | tf_op jit(solution)/shard_map/ppermute | solution.py:151
  46.3 1.8 %collective-permute-done.17 = bf16[64,576]{1,0:T(8,128)(2,1)S(1)} collective-permute-done((bf16[64,576]{1,0:T(8,128)(2,1)S(1)}, bf16[64,576]{1,0:T(8,128)(2,1)S(1)}, u32[]{:S(2)}, u32[]{:S(2)}) %collective-permute-start.17) | collective-permute-done | bytes 73760 | tf_op jit(solution)/shard_map/ppermute | solution.py:151
  48.2 2.8 %collective-permute-start.18 = (bf16[64,576]{1,0:T(8,128)(2,1)S(1)}, bf16[64,576]{1,0:T(8,128)(2,1)S(1)}, u32[]{:S(2)}, u32[]{:S(2)}) collective-permute-start(bf16[64,576]{1,0:T(8,128)(2,1)S(1)} %get-tuple-element.14), channel_id=1, source_target_pairs={{0,6},{1,7},{2,4},{3,5},{4,2},{5,3},{6,0},{7,1},{8,14},{9,15},{10,... | collective-permute-start | bytes 221192 | tf_op jit(solution)/shard_map/ppermute | solution.py:151
  51.1 1.5 %collective-permute-start.20 = (bf16[64,576]{1,0:T(8,128)(2,1)S(1)}, bf16[64,576]{1,0:T(8,128)(2,1)S(1)}, u32[]{:S(2)}, u32[]{:S(2)}) collective-permute-start(bf16[64,576]{1,0:T(8,128)(2,1)S(1)} %get-tuple-element.16), channel_id=1, source_target_pairs={{0,4},{1,5},{2,6},{3,7},{4,0},{5,1},{6,2},{7,3},{8,12},{9,13},{10,... | collective-permute-start | bytes 221192 | tf_op jit(solution)/shard_map/ppermute | solution.py:151
  52.6 3.2 %query_grad.1 = bf16[576,512]{1,0:T(8,128)(2,1)} custom-call(bf16[1024,576]{1,0:T(8,128)(2,1)} %get-tuple-element.6.keys_ref, bf16[1024,512]{1,0:T(8,128)(2,1)} %get-tuple-element.7.score_grad_ref), custom_call_target="tpu_custom_call" | custom-call | tf_op jit(solution)/shard_map/query_grad/pallas_call | solution.py:134
  56.0 0.8 %collective-permute-done.22 = bf16[64,576]{1,0:T(8,128)(2,1)S(1)} collective-permute-done((bf16[64,576]{1,0:T(8,128)(2,1)S(1)}, bf16[64,576]{1,0:T(8,128)(2,1)S(1)}, u32[]{:S(2)}, u32[]{:S(2)}) %collective-permute-start.22) | collective-permute-done | bytes 73760 | tf_op jit(solution)/shard_map/ppermute | solution.py:151
  56.8 0.7 %add_convert_fusion = bf16[64,576]{1,0:T(8,128)(2,1)} fusion(bf16[64,576]{1,0:T(8,128)(2,1)S(1)} %collective-permute-done.22, bf16[64,576]{1,0:T(8,128)(2,1)S(1)} %collective-permute-done.20, bf16[64,576]{1,0:T(8,128)(2,1)S(1)} %collective-permute-done.18, bf16[64,576]{1,0:T(8,128)(2,1)S(1)} %collective-permute-done.16, bf16[64,576]{1,0:T(8,128)(2,1)S(1)} %copy.15, ...), kind=kLoop, calls=%fused_computation | loop fusion | flops 405504 | bytes 589824 | tf_op jit(solution)/shard_map/convert_element_type | solution.py:212
  (62 shorter events, 2.6 us)
Async XLA Ops:
  0.6 8.7 %collective-permute-start.5 = (bf16[64,576]{1,0:T(8,128)(2,1)}, bf16[64,576]{1,0:T(8,128)(2,1)S(1)}, u32[]{:S(2)}, u32[]{:S(2)}) collective-permute-start(bf16[64,576]{1,0:T(8,128)(2,1)} %refs_0_.1), channel_id=1, source_target_pairs={{0,6},{1,7},{2,4},{3,5},{4,2},{5,3},{6,0},{7,1},{8,14},{9,15},{10,... | collective-permute-start | bytes 221192 | tf_op jit(solution)/shard_map/ppermute | solution.py:151
  5.8 7.1 %collective-permute-start.3 = (bf16[64,576]{1,0:T(8,128)(2,1)}, bf16[64,576]{1,0:T(8,128)(2,1)S(1)}, u32[]{:S(2)}, u32[]{:S(2)}) collective-permute-start(bf16[64,576]{1,0:T(8,128)(2,1)} %refs_0_.1), channel_id=1, source_target_pairs={{0,4},{1,5},{2,6},{3,7},{4,0},{5,1},{6,2},{7,3},{8,12},{9,13},{10,... | collective-permute-start | bytes 221192 | tf_op jit(solution)/shard_map/ppermute | solution.py:151
  5.8 8.6 %collective-permute-start.1 = (bf16[64,576]{1,0:T(8,128)(2,1)}, bf16[64,576]{1,0:T(8,128)(2,1)S(1)}, u32[]{:S(2)}, u32[]{:S(2)}) collective-permute-start(bf16[64,576]{1,0:T(8,128)(2,1)} %refs_0_.1), channel_id=1, source_target_pairs={{0,2},{1,3},{2,0},{3,1},{4,6},{5,7},{6,4},{7,5},{8,10},{9,11},{10,... | collective-permute-start | bytes 221192 | tf_op jit(solution)/shard_map/ppermute | solution.py:151
  6.4 9.2 %collective-permute-start = (bf16[64,576]{1,0:T(8,128)(2,1)}, bf16[64,576]{1,0:T(8,128)(2,1)S(1)}, u32[]{:S(2)}, u32[]{:S(2)}) collective-permute-start(bf16[64,576]{1,0:T(8,128)(2,1)} %refs_0_.1), channel_id=1, source_target_pairs={{0,1},{1,0},{2,3},{3,2},{4,5},{5,4},{6,7},{7,6},{8,9},{9,8},{10,11... | collective-permute-start | bytes 221192 | tf_op jit(solution)/shard_map/ppermute | solution.py:151
  8.1 8.2 %collective-permute-start.7 = (bf16[64,576]{1,0:T(8,128)(2,1)}, bf16[64,576]{1,0:T(8,128)(2,1)S(1)}, u32[]{:S(2)}, u32[]{:S(2)}) collective-permute-start(bf16[64,576]{1,0:T(8,128)(2,1)} %refs_0_.1), channel_id=1, source_target_pairs={{0,8},{1,9},{2,10},{3,11},{4,12},{5,13},{6,14},{7,15},{16,24},{17,... | collective-permute-start | bytes 221192 | tf_op jit(solution)/shard_map/ppermute | solution.py:146
  9.4 15.9 %copy-start.1 = (bf16[64,576]{1,0:T(8,128)(2,1)}, bf16[64,576]{1,0:T(8,128)(2,1)S(1)}, u32[]{:S(2)}) copy-start(bf16[64,576]{1,0:T(8,128)(2,1)S(1)} %collective-permute-done.5.refs_6_) | copy-start | bytes 221188
  9.4 8.4 %collective-permute-start.13 = (bf16[64,576]{1,0:T(8,128)(2,1)S(1)}, bf16[64,576]{1,0:T(8,128)(2,1)S(1)}, u32[]{:S(2)}, u32[]{:S(2)}) collective-permute-start(bf16[64,576]{1,0:T(8,128)(2,1)S(1)} %collective-permute-done.5.refs_6_), channel_id=1, source_target_pairs={{0,8},{1,9},{2,10},{3,11},{4,12},{5,13},{6,14},{7,15},{16,24},{17,... | collective-permute-start | bytes 221192 | tf_op jit(solution)/shard_map/ppermute | solution.py:146
  12.8 12.4 %copy-start.2 = (bf16[64,576]{1,0:T(8,128)(2,1)}, bf16[64,576]{1,0:T(8,128)(2,1)S(1)}, u32[]{:S(2)}) copy-start(bf16[64,576]{1,0:T(8,128)(2,1)S(1)} %collective-permute-done.3.refs_4_) | copy-start | bytes 221188
  12.8 6.2 %collective-permute-start.6 = (bf16[64,576]{1,0:T(8,128)(2,1)S(1)}, bf16[64,576]{1,0:T(8,128)(2,1)S(1)}, u32[]{:S(2)}, u32[]{:S(2)}) collective-permute-start(bf16[64,576]{1,0:T(8,128)(2,1)S(1)} %collective-permute-done.5.refs_6_), channel_id=1, source_target_pairs={{0,1},{1,0},{2,3},{3,2},{4,5},{5,4},{6,7},{7,6},{8,9},{9,8},{10,11... | collective-permute-start | bytes 221192 | tf_op jit(solution)/shard_map/ppermute | solution.py:151
  14.3 10.9 %copy-start.3 = (bf16[64,576]{1,0:T(8,128)(2,1)}, bf16[64,576]{1,0:T(8,128)(2,1)S(1)}, u32[]{:S(2)}) copy-start(bf16[64,576]{1,0:T(8,128)(2,1)S(1)} %collective-permute-done.1.refs_2_) | copy-start | bytes 221188
  14.3 6.0 %collective-permute-start.11 = (bf16[64,576]{1,0:T(8,128)(2,1)S(1)}, bf16[64,576]{1,0:T(8,128)(2,1)S(1)}, u32[]{:S(2)}, u32[]{:S(2)}) collective-permute-start(bf16[64,576]{1,0:T(8,128)(2,1)S(1)} %collective-permute-done.3.refs_4_), channel_id=1, source_target_pairs={{0,8},{1,9},{2,10},{3,11},{4,12},{5,13},{6,14},{7,15},{16,24},{17,... | collective-permute-start | bytes 221192 | tf_op jit(solution)/shard_map/ppermute | solution.py:146
  15.6 9.6 %copy-start.4 = (bf16[64,576]{1,0:T(8,128)(2,1)}, bf16[64,576]{1,0:T(8,128)(2,1)S(1)}, u32[]{:S(2)}) copy-start(bf16[64,576]{1,0:T(8,128)(2,1)S(1)} %collective-permute-done.refs_1_) | copy-start | bytes 221188
  15.7 6.0 %collective-permute-start.4 = (bf16[64,576]{1,0:T(8,128)(2,1)S(1)}, bf16[64,576]{1,0:T(8,128)(2,1)S(1)}, u32[]{:S(2)}, u32[]{:S(2)}) collective-permute-start(bf16[64,576]{1,0:T(8,128)(2,1)S(1)} %collective-permute-done.3.refs_4_), channel_id=1, source_target_pairs={{0,1},{1,0},{2,3},{3,2},{4,5},{5,4},{6,7},{7,6},{8,9},{9,8},{10,11... | collective-permute-start | bytes 221192 | tf_op jit(solution)/shard_map/ppermute | solution.py:151
  16.3 9.0 %copy-start.5 = (bf16[64,576]{1,0:T(8,128)(2,1)}, bf16[64,576]{1,0:T(8,128)(2,1)S(1)}, u32[]{:S(2)}) copy-start(bf16[64,576]{1,0:T(8,128)(2,1)S(1)} %collective-permute-done.7.refs_8_) | copy-start | bytes 221188
  16.3 6.8 %collective-permute-start.2 = (bf16[64,576]{1,0:T(8,128)(2,1)S(1)}, bf16[64,576]{1,0:T(8,128)(2,1)S(1)}, u32[]{:S(2)}, u32[]{:S(2)}) collective-permute-start(bf16[64,576]{1,0:T(8,128)(2,1)S(1)} %collective-permute-done.1.refs_2_), channel_id=1, source_target_pairs={{0,1},{1,0},{2,3},{3,2},{4,5},{5,4},{6,7},{7,6},{8,9},{9,8},{10,11... | collective-permute-start | bytes 221192 | tf_op jit(solution)/shard_map/ppermute | solution.py:151
  17.8 7.5 %copy-start.6 = (bf16[64,576]{1,0:T(8,128)(2,1)}, bf16[64,576]{1,0:T(8,128)(2,1)S(1)}, u32[]{:S(2)}) copy-start(bf16[64,576]{1,0:T(8,128)(2,1)S(1)} %collective-permute-done.13.refs_14_) | copy-start | bytes 221188
  17.8 7.2 %collective-permute-start.9 = (bf16[64,576]{1,0:T(8,128)(2,1)S(1)}, bf16[64,576]{1,0:T(8,128)(2,1)S(1)}, u32[]{:S(2)}, u32[]{:S(2)}) collective-permute-start(bf16[64,576]{1,0:T(8,128)(2,1)S(1)} %collective-permute-done.1.refs_2_), channel_id=1, source_target_pairs={{0,8},{1,9},{2,10},{3,11},{4,12},{5,13},{6,14},{7,15},{16,24},{17,... | collective-permute-start | bytes 221192 | tf_op jit(solution)/shard_map/ppermute | solution.py:146
  19.1 6.2 %copy-start.7 = (bf16[64,576]{1,0:T(8,128)(2,1)}, bf16[64,576]{1,0:T(8,128)(2,1)S(1)}, u32[]{:S(2)}) copy-start(bf16[64,576]{1,0:T(8,128)(2,1)S(1)} %collective-permute-done.6.refs_7_) | copy-start | bytes 221188
  19.1 5.9 %collective-permute-start.8 = (bf16[64,576]{1,0:T(8,128)(2,1)S(1)}, bf16[64,576]{1,0:T(8,128)(2,1)S(1)}, u32[]{:S(2)}, u32[]{:S(2)}) collective-permute-start(bf16[64,576]{1,0:T(8,128)(2,1)S(1)} %collective-permute-done.refs_1_), channel_id=1, source_target_pairs={{0,8},{1,9},{2,10},{3,11},{4,12},{5,13},{6,14},{7,15},{16,24},{17,... | collective-permute-start | bytes 221192 | tf_op jit(solution)/shard_map/ppermute | solution.py:146
  20.4 4.9 %copy-start.8 = (bf16[64,576]{1,0:T(8,128)(2,1)}, bf16[64,576]{1,0:T(8,128)(2,1)S(1)}, u32[]{:S(2)}) copy-start(bf16[64,576]{1,0:T(8,128)(2,1)S(1)} %collective-permute-done.11.refs_12_) | copy-start | bytes 221188
  20.4 4.6 %collective-permute-start.14 = (bf16[64,576]{1,0:T(8,128)(2,1)S(1)}, bf16[64,576]{1,0:T(8,128)(2,1)S(1)}, u32[]{:S(2)}, u32[]{:S(2)}) collective-permute-start(bf16[64,576]{1,0:T(8,128)(2,1)S(1)} %collective-permute-done.6.refs_7_), channel_id=1, source_target_pairs={{0,8},{1,9},{2,10},{3,11},{4,12},{5,13},{6,14},{7,15},{16,24},{17,... | collective-permute-start | bytes 221192 | tf_op jit(solution)/shard_map/ppermute | solution.py:146
  21.7 3.3 %collective-permute-start.12 = (bf16[64,576]{1,0:T(8,128)(2,1)S(1)}, bf16[64,576]{1,0:T(8,128)(2,1)S(1)}, u32[]{:S(2)}, u32[]{:S(2)}) collective-permute-start(bf16[64,576]{1,0:T(8,128)(2,1)S(1)} %collective-permute-done.4.refs_5_), channel_id=1, source_target_pairs={{0,8},{1,9},{2,10},{3,11},{4,12},{5,13},{6,14},{7,15},{16,24},{17,... | collective-permute-start | bytes 221192 | tf_op jit(solution)/shard_map/ppermute | solution.py:146
  23.0 2.2 %collective-permute-start.10 = (bf16[64,576]{1,0:T(8,128)(2,1)S(1)}, bf16[64,576]{1,0:T(8,128)(2,1)S(1)}, u32[]{:S(2)}, u32[]{:S(2)}) collective-permute-start(bf16[64,576]{1,0:T(8,128)(2,1)S(1)} %collective-permute-done.2.refs_3_), channel_id=1, source_target_pairs={{0,8},{1,9},{2,10},{3,11},{4,12},{5,13},{6,14},{7,15},{16,24},{17,... | collective-permute-start | bytes 221192 | tf_op jit(solution)/shard_map/ppermute | solution.py:146
  33.0 6.1 %copy-start = (f32[512,576]{1,0:T(8,128)S(1)}, f32[512,576]{1,0:T(8,128)}, u32[]{:S(2)}) copy-start(f32[512,576]{1,0:T(8,128)} %get-tuple-element.8) | copy-start | bytes 3538948
  33.0 5.2 %collective-permute-start.15 = (bf16[512,576]{0,1:T(8,128)(2,1)S(1)}, bf16[512,576]{0,1:T(8,128)(2,1)S(1)}, u32[]{:S(2)}, u32[]{:S(2)}) collective-permute-start(bf16[512,576]{0,1:T(8,128)(2,1)S(1)} %copy.6), channel_id=1, source_target_pairs={{8,0},{9,1},{10,2},{11,3},{12,4},{13,5},{14,6},{15,7},{24,16},{25,... | collective-permute-start | bytes 1769480 | tf_op jit(solution)/shard_map/ppermute | solution.py:146
  39.2 5.4 %collective-permute-start.21 = (bf16[64,576]{1,0:T(8,128)(2,1)S(1)}, bf16[64,576]{1,0:T(8,128)(2,1)S(1)}, u32[]{:S(2)}, u32[]{:S(2)}) collective-permute-start(bf16[64,576]{1,0:T(8,128)(2,1)S(1)} %get-tuple-element.11), channel_id=1, source_target_pairs={{0,1},{1,0},{2,3},{3,2},{4,5},{5,4},{6,7},{7,6},{8,9},{9,8},{10,11... | collective-permute-start | bytes 221192 | tf_op jit(solution)/shard_map/ppermute | solution.py:151
  39.8 6.5 %collective-permute-start.19 = (bf16[64,576]{1,0:T(8,128)(2,1)S(1)}, bf16[64,576]{1,0:T(8,128)(2,1)S(1)}, u32[]{:S(2)}, u32[]{:S(2)}) collective-permute-start(bf16[64,576]{1,0:T(8,128)(2,1)S(1)} %get-tuple-element.12), channel_id=1, source_target_pairs={{0,1},{1,0},{2,3},{3,2},{4,5},{5,4},{6,7},{7,6},{8,9},{9,8},{10,11... | collective-permute-start | bytes 221192 | tf_op jit(solution)/shard_map/ppermute | solution.py:151
  41.3 6.8 %collective-permute-start.17 = (bf16[64,576]{1,0:T(8,128)(2,1)S(1)}, bf16[64,576]{1,0:T(8,128)(2,1)S(1)}, u32[]{:S(2)}, u32[]{:S(2)}) collective-permute-start(bf16[64,576]{1,0:T(8,128)(2,1)S(1)} %get-tuple-element.13), channel_id=1, source_target_pairs={{0,1},{1,0},{2,3},{3,2},{4,5},{5,4},{6,7},{7,6},{8,9},{9,8},{10,11... | collective-permute-start | bytes 221192 | tf_op jit(solution)/shard_map/ppermute | solution.py:151
  42.3 13.7 %collective-permute-start.16 = (bf16[64,576]{1,0:T(8,128)(2,1)S(1)}, bf16[64,576]{1,0:T(8,128)(2,1)S(1)}, u32[]{:S(2)}, u32[]{:S(2)}) collective-permute-start(bf16[64,576]{1,0:T(8,128)(2,1)S(1)} %get-tuple-element.10), channel_id=1, source_target_pairs={{0,1},{1,0},{2,3},{3,2},{4,5},{5,4},{6,7},{7,6},{8,9},{9,8},{10,11... | collective-permute-start | bytes 221192 | tf_op jit(solution)/shard_map/ppermute | solution.py:151
  48.2 7.8 %collective-permute-start.18 = (bf16[64,576]{1,0:T(8,128)(2,1)S(1)}, bf16[64,576]{1,0:T(8,128)(2,1)S(1)}, u32[]{:S(2)}, u32[]{:S(2)}) collective-permute-start(bf16[64,576]{1,0:T(8,128)(2,1)S(1)} %get-tuple-element.14), channel_id=1, source_target_pairs={{0,6},{1,7},{2,4},{3,5},{4,2},{5,3},{6,0},{7,1},{8,14},{9,15},{10,... | collective-permute-start | bytes 221192 | tf_op jit(solution)/shard_map/ppermute | solution.py:151
  50.9 5.9 %collective-permute-start.22 = (bf16[64,576]{1,0:T(8,128)(2,1)S(1)}, bf16[64,576]{1,0:T(8,128)(2,1)S(1)}, u32[]{:S(2)}, u32[]{:S(2)}) collective-permute-start(bf16[64,576]{1,0:T(8,128)(2,1)S(1)} %get-tuple-element.15), channel_id=1, source_target_pairs={{0,2},{1,3},{2,0},{3,1},{4,6},{5,7},{6,4},{7,5},{8,10},{9,11},{10,... | collective-permute-start | bytes 221192 | tf_op jit(solution)/shard_map/ppermute | solution.py:151
  51.1 5.7 %collective-permute-start.20 = (bf16[64,576]{1,0:T(8,128)(2,1)S(1)}, bf16[64,576]{1,0:T(8,128)(2,1)S(1)}, u32[]{:S(2)}, u32[]{:S(2)}) collective-permute-start(bf16[64,576]{1,0:T(8,128)(2,1)S(1)} %get-tuple-element.16), channel_id=1, source_target_pairs={{0,4},{1,5},{2,6},{3,7},{4,0},{5,1},{6,2},{7,3},{8,12},{9,13},{10,... | collective-permute-start | bytes 221192 | tf_op jit(solution)/shard_map/ppermute | solution.py:151
  (7 other events, 9.2 us)

commit v2 on v0

v2 whole, which is shorter than its diff:
```python
import functools

import jax
import jax.numpy as jnp
from jax import lax
from jax.experimental import pallas as pl
from jax.experimental.pallas import tpu as pltpu
from jax.sharding import PartitionSpec as P


score_scale = 192.0 ** (-0.5)
masked_score = -1e30
most_pieces = 16
kernel_room = 24 * 2**20
f32 = jnp.float32
bf16 = jnp.bfloat16


def dot_nn(a, b):
    return lax.dot_general(a, b, (((1,), (0,)), ((), ())), preferred_element_type=f32)


def dot_nt(a, b):
    return lax.dot_general(a, b, (((1,), (1,)), ((), ())), preferred_element_type=f32)


def dot_tn(a, b):
    return lax.dot_general(a, b, (((0,), (0,)), ((), ())), preferred_element_type=f32)


def tiling(block_len):
    tile = min(256, block_len)
    return tile, block_len // tile


def from_lane(acc, value, lane, op):
    if acc is None:
        return value
    if lane == 0:
        return op(acc, value)
    return jnp.concatenate([acc[:, :lane], op(acc[:, lane:], value)], axis=1)


def place(scalars, ids, refs, keys_ref):
    piece_len = keys_ref.shape[0] // sum(len(i) for i in ids)
    for group, ref in zip(ids, refs):
        for q, m in enumerate(group):
            start = pl.multiple_of((scalars[0] ^ m) * piece_len, piece_len)
            keys_ref[pl.ds(start, piece_len), :] = ref[q * piece_len : (q + 1) * piece_len, :]


def own_kernel(ids, scalars, query_ref, grad_ref, *refs):
    pieces, (keys_ref, score_ref, prob_grad_ref, peak_ref) = refs[:-4], refs[-4:]
    place(scalars, ids, pieces, keys_ref)
    block_len, rank_width = grad_ref.shape
    tile, tiles = tiling(block_len)
    peak = None
    for c in range(tiles):
        rows, lane = pl.ds(c * tile, tile), c * tile
        keys = keys_ref[rows, :]
        scores = dot_nn(keys, query_ref[:, lane:]) * score_scale
        key_pos = lax.broadcasted_iota(jnp.int32, scores.shape, 0)
        token_pos = lax.broadcasted_iota(jnp.int32, scores.shape, 1)
        scores = jnp.where(key_pos <= token_pos, scores, masked_score)
        score_ref[rows, lane:] = scores
        peak = from_lane(peak, jnp.max(scores, axis=0, keepdims=True), lane, jnp.maximum)
        prob_grad_ref[rows, lane:] = dot_nt(keys[:, :rank_width], grad_ref[lane:, :])
    peak_ref[...] = peak


def joint_kernel(ids, scalars, first_ref, query_ref, grad_ref, own_score_ref, own_prob_grad_ref,
                 own_peak_ref, *refs):
    pieces = refs[: len(ids)]
    (keys_ref, prev_ref, prev_sg_ref, own_sg_ref, own_probs_ref, prev_score_ref,
     prev_prob_grad_ref, prev_probs_ref) = refs[len(ids) :]
    block_len, rank_width = grad_ref.shape
    tile, tiles = tiling(block_len)

    def run(with_prev):
        parts = []
        if with_prev:
            for c in range(tiles):
                parts.append((pl.ds(c * tile, tile), 0, prev_score_ref, prev_prob_grad_ref,
                              prev_probs_ref, prev_sg_ref))
        for c in range(tiles):
            parts.append((pl.ds(c * tile, tile), c * tile, own_score_ref, own_prob_grad_ref,
                          own_probs_ref, own_sg_ref))
        peak = own_peak_ref[...]
        if with_prev:
            place(scalars, ids, pieces, keys_ref)
            first = first_ref[...] - (scalars[1] - 1) * block_len
            for c in range(tiles):
                rows = pl.ds(c * tile, tile)
                keys = keys_ref[rows, :]
                scores = dot_nn(keys, query_ref[...]) * score_scale
                key_pos = lax.broadcasted_iota(jnp.int32, scores.shape, 0) + c * tile
                scores = jnp.where(key_pos >= first, scores, masked_score)
                prev_score_ref[rows, :] = scores
                peak = jnp.maximum(peak, jnp.max(scores, axis=0, keepdims=True))
                prev_prob_grad_ref[rows, :] = dot_nt(keys[:, :rank_width], grad_ref[...])
        total = None
        for rows, lane, score_ref, _, _, _ in parts:
            lifted = jnp.exp(score_ref[rows, lane:] - peak[:, lane:])
            score_ref[rows, lane:] = lifted
            total = from_lane(total, jnp.sum(lifted, axis=0, keepdims=True), lane, jnp.add)
        inverse = 1.0 / total
        delta = None
        for rows, lane, score_ref, prob_grad_ref, probs_ref, _ in parts:
            probs = (score_ref[rows, lane:] * inverse[:, lane:]).astype(bf16)
            probs_ref[rows, lane:] = probs
            term = jnp.sum(probs.astype(f32) * prob_grad_ref[rows, lane:], axis=0, keepdims=True)
            delta = from_lane(delta, term, lane, jnp.add)
        for rows, lane, _, prob_grad_ref, probs_ref, sg_ref in parts:
            probs = probs_ref[rows, lane:].astype(f32)
            sg = probs * (prob_grad_ref[rows, lane:] - delta[:, lane:]) * score_scale
            sg_ref[rows, lane:] = sg.astype(bf16)
        if with_prev:
            for c in range(tiles):
                rows = pl.ds(c * tile, tile)
                store_latents(prev_ref, rows, prev_sg_ref[rows, :], prev_probs_ref[rows, :],
                              query_ref[...], grad_ref[...])
        else:
            prev_ref[...] = jnp.zeros(prev_ref.shape, prev_ref.dtype)

    @pl.when(scalars[1] > 0)
    def _():
        run(True)

    @pl.when(scalars[1] == 0)
    def _():
        run(False)


def store_latents(out_ref, rows, score_grad, probs, query_t, grad_rows):
    width, rank_width = query_t.shape[0], grad_rows.shape[1]
    latent_part = dot_nt(score_grad, query_t)
    value_part = dot_nn(probs, grad_rows)
    out_ref[rows, :rank_width] = (latent_part[:, :rank_width] + value_part).astype(out_ref.dtype)
    rest = latent_part[:, rank_width:]
    pad = out_ref.shape[1] - width
    if pad:
        rest = jnp.concatenate([rest, jnp.zeros((rest.shape[0], pad), f32)], axis=1)
    out_ref[rows, rank_width:] = rest.astype(out_ref.dtype)


def own_latents_kernel(query_ref, grad_ref, own_sg_ref, own_probs_ref, out_ref):
    tile, tiles = tiling(grad_ref.shape[0])
    for c in range(tiles):
        rows, lane = pl.ds(c * tile, tile), c * tile
        store_latents(out_ref, rows, own_sg_ref[rows, lane:], own_probs_ref[rows, lane:],
                      query_ref[:, lane:], grad_ref[lane:, :])


def chunks_kernel(groups, scalars, own_ref, later_ref, *outs):
    piece_len = own_ref.shape[0] // len(outs)

    def run(with_later):
        for m, out in enumerate(outs):
            start = pl.multiple_of((scalars[0] ^ m) * piece_len, piece_len)
            rows = own_ref[pl.ds(start, piece_len), :]
            if with_later:
                rows = rows + later_ref[pl.ds(start, piece_len), :].astype(f32)
            out[...] = rows.astype(out.dtype)

    @pl.when(scalars[1] < groups - 1)
    def _():
        run(True)

    @pl.when(scalars[1] == groups - 1)
    def _():
        run(False)


def query_grad_kernel(scalars, prev_keys_ref, own_keys_ref, prev_sg_ref, own_sg_ref, out_ref):
    tile, tiles = tiling(own_sg_ref.shape[0])

    def run(with_prev):
        for c in range(tiles):
            lanes = slice(c * tile, (c + 1) * tile)
            seen = (c + 1) * tile
            acc = dot_tn(own_keys_ref[:seen, :], own_sg_ref[:seen, lanes])
            if with_prev:
                acc = acc + dot_tn(prev_keys_ref[...], prev_sg_ref[:, lanes])
            out_ref[:, lanes] = acc.astype(bf16)

    @pl.when(scalars[1] > 0)
    def _():
        run(True)

    @pl.when(scalars[1] == 0)
    def _():
        run(False)


def add_kernel(*refs):
    total = refs[0][...].astype(f32)
    for ref in refs[1:-1]:
        total = total + ref[...].astype(f32)
    out_ref = refs[-1]
    out_ref[...] = total[:, : out_ref.shape[1]].astype(bf16)


def added(terms, width=None):
    rows, cols = terms[0].shape
    return call(add_kernel, [((rows, width or cols), bf16)], terms)[0]


def on_chip(x):
    return pltpu.with_memory_space_constraint(x, pltpu.VMEM)


def call(kernel, outs, args, scratch=(), scalars=None):
    specs = [pl.BlockSpec(memory_space=pltpu.VMEM)] * len(args)
    args = [on_chip(x) for x in args]
    if scalars is not None:
        specs = [pl.BlockSpec(memory_space=pltpu.SMEM)] + specs
        args = [scalars] + args
    result = pl.pallas_call(
        kernel,
        out_shape=tuple(pltpu.VMEM(s, d) for s, d in outs),
        in_specs=specs,
        out_specs=tuple(pl.BlockSpec(memory_space=pltpu.VMEM) for _ in outs),
        scratch_shapes=[pltpu.VMEM(s, d) for s, d in scratch],
        compiler_params=pltpu.CompilerParams(vmem_limit_bytes=kernel_room),
    )(*args)
    return result


def rotated(shard, axis, by):
    count = lax.axis_size(axis)
    return lax.ppermute(shard, axis, [(i, (i + by) % count) for i in range(count)])


def swapped(shard, mask):
    count = lax.axis_size("blk")
    return lax.ppermute(shard, "blk", [(i, i ^ mask) for i in range(count)])


def top_bit(m):
    return 1 << (m.bit_length() - 1)


def routes(count):
    direct = [m for m in range(2, count) if m == top_bit(m)] + [1]
    relayed = [m for m in range(1, count) if m != top_bit(m)]
    relayed.sort(key=lambda m: (top_bit(m), -((m - top_bit(m)) & 1), -m))
    return direct, relayed


def shards(queries, latents, out_grad, first_key):
    block_len, head_local, width = queries.shape
    count = lax.axis_size("blk")
    groups = lax.axis_size("grp")
    by_swaps = routed(count)
    blk_index = lax.axis_index("blk") if by_swaps else jnp.zeros((), jnp.int32)
    scalars = jnp.stack([blk_index, lax.axis_index("grp")]).astype(jnp.int32)
    padded = -(-width // 128) * 128
    first_row = first_key.reshape(1, block_len)

    if by_swaps:
        direct, relayed = routes(count)
        pieces = {0: latents}
        for m in direct:
            pieces[m] = swapped(latents, m)
        early = [0] + direct
        prev_early = rotated(jnp.concatenate([pieces[m] for m in early], axis=0), "grp", 1)
        for m in relayed:
            pieces[m] = swapped(pieces[top_bit(m)], m - top_bit(m))
        prev_late = rotated(jnp.concatenate([pieces[m] for m in relayed], axis=0), "grp", 1)
        own_ids = tuple((m,) for m in range(count))
        own = [pieces[m] for m in range(count)]
        prev_ids = (tuple(early), tuple(relayed))
        prev = [prev_early, prev_late]
    else:
        own_ids = prev_ids = ((0,),)
        own = [lax.all_gather(latents, "blk", axis=0, tiled=True)]
        prev = [rotated(own[0], "grp", 1)]

    square = (block_len, block_len)
    query_work = []
    own_part = prev_part = None
    for h in range(head_local):
        query_t, grad_rows = queries[:, h, :].T, out_grad[:, h, :]
        own_keys, own_score, own_prob_grad, own_peak = call(
            functools.partial(own_kernel, own_ids),
            [((block_len, width), bf16), (square, f32), (square, f32), ((1, block_len), f32)],
            [query_t, grad_rows] + own, scalars=scalars,
        )
        prev_keys, prev_h, prev_sg, own_sg, own_probs = call(
            functools.partial(joint_kernel, prev_ids),
            [((block_len, width), bf16), ((block_len, padded), bf16), (square, bf16),
             (square, bf16), (square, bf16)],
            [first_row, query_t, grad_rows, own_score, own_prob_grad, own_peak] + prev,
            scratch=[(square, f32), (square, f32), (square, bf16)], scalars=scalars,
        )
        (own_h,) = call(own_latents_kernel, [((block_len, padded), f32)],
                        [query_t, grad_rows, own_sg, own_probs])
        query_work.append((prev_keys, own_keys, prev_sg, own_sg))
        own_part = own_h if h == 0 else own_part + own_h
        prev_part = prev_h if h == 0 else prev_part.astype(f32) + prev_h.astype(f32)
    later = rotated(prev_part.astype(bf16), "grp", -1)

    pieces_out = count if by_swaps else 1
    piece = (block_len // pieces_out, padded)
    kinds = [f32 if m == 0 or m == top_bit(m) and m > 1 else bf16 for m in range(pieces_out)]
    chunks = call(functools.partial(chunks_kernel, groups),
                  [(piece, kind) for kind in kinds], [own_part, later], scalars=scalars)
    if by_swaps:
        sums = {m: [chunks[m]] for m in direct}
        for m in sorted(relayed, key=lambda m: (-top_bit(m), -(m - top_bit(m) & 1), -m)):
            sums[top_bit(m)].append(swapped(chunks[m], m - top_bit(m)))
        last = [chunks[0]]
        for m in direct:
            sent = chunks[m] if len(sums[m]) == 1 else added(sums[m])
            last.append(swapped(sent, m))
        total = added(last, width)
    else:
        total = lax.psum_scatter(chunks[0], "blk", scatter_dimension=0, tiled=True)
        total = total[:, :width].astype(bf16)
    query_parts = [
        call(query_grad_kernel, [((width, block_len), bf16)], list(work),
             scalars=scalars)[0].T
        for work in query_work
    ]
    return (jnp.stack(query_parts, axis=1), total)


def routed(count):
    return 2 <= count <= most_pieces and count & (count - 1) == 0


def solution(mesh):
    placed = (
        P(("rep", "grp"), "blk", None),
        P(("rep", "grp", "blk"), None),
        P(("rep", "grp"), "blk", None),
        P(("rep", "grp")),
    )

    return jax.shard_map(
        shards,
        mesh=mesh,
        in_specs=placed,
        out_specs=(P(("rep", "grp"), "blk", None), P(("rep", "grp", "blk"), None)),
        check_vma=False,
    )
```

time: 132 us -> 42.4 us (0.32)
  waiting for transfers between devices: 66.6 us -> 7.07 us
  blocking collectives: 33.8 us -> 0 us
  starting transfers between devices: 2.66 us -> 27 us
  between operations: 14.2 us -> 0.76 us
  matrix products: 7.27 us -> 0 us
  Pallas kernels: 0 us -> 4.88 us
  local copies, waits for them, and re-layouts: 4.87 us -> 1.47 us
  other arithmetic: 2.68 us -> 1.03 us
    unnamed x2 -> x0, waiting for transfers between devices: 63.4 us -> none
    all_gather x1 -> x0, blocking collectives: 33.8 us -> none  [shards(): own_block = lax.all_gather(latents, 'blk', axis=0, tiled=True)]
    ppermute x2 -> x17, starting transfers between devices: 2.62 us -> 27 us  [the longest x14 24.1 us: swapped(): return lax.ppermute(shard, 'blk', [(i, i ^ mask) for i in range(count)])]
    dot_general x6 -> x0, matrix products: 7.27 us -> none  [the longest x1 2.73 us: attend_grads(): jnp.dot(score_grad, key_rows, preferred_element_type=jnp.float32)]
    pallas_call x0 -> x8, Pallas kernels: none -> 4.88 us  [call(): pl.pallas_call(kernel, out_shape=tuple((pltpu.VMEM(s, d) for s, d in outs...]
    ppermute x2 -> x17, waiting for transfers between devices: 3.14 us -> 7.07 us  [the longest x14 5.82 us: swapped(): return lax.ppermute(shard, 'blk', [(i, i ^ mask) for i in range(count)])]
    unnamed x14 -> x10, local copies, waits for them, and re-layouts: 4.32 us -> 1.47 us
  transfers between devices with their start and end apart: 3 -> 17, of which waited for: 3 -> 9; matrix products, arithmetic and copies ran while one was open for 3% -> 4% of each run, Pallas kernels for 0% -> 7%
where the time goes in v2:
time: 42.4 us; the launch traced here: 42.2 us
  starting transfers between devices  27 us (64%)
  waiting for transfers between devices  7.07 us (17%)
  Pallas kernels  4.88 us (12%)
  local copies, waits for them, and re-layouts  1.47 us (3%)
  other arithmetic  1.03 us (2%)
  between operations  0.76 us (2%)
    ppermute x14, starting transfers between devices, swapped(): return lax.ppermute(shard, 'blk', [(i, i ^ mask) for i in range(count)])  24.1 us
    ppermute x14, waiting for transfers between devices, swapped(): return lax.ppermute(shard, 'blk', [(i, i ^ mask) for i in range(count)])  5.82 us
    pallas_call x8, Pallas kernels, call(): pl.pallas_call(kernel, out_shape=tuple((pltpu.VMEM(s, d) for s, d in outs...  4.88 us
    ppermute x3, starting transfers between devices, rotated(): lax.ppermute(shard, axis, [(i, (i + by) % count) for i in range(count)])  2.84 us
    unnamed x10, local copies, waits for them, and re-layouts  1.47 us
    ppermute x3, waiting for transfers between devices, rotated(): lax.ppermute(shard, axis, [(i, (i + by) % count) for i in range(count)])  1.26 us
    concatenate x1, other arithmetic, shards(): jnp.concatenate([pieces[m] for m in early], axis=0)  0.92 us
  transfers between devices with their start and end apart: 17, of which 9 were waited for; matrix products, arithmetic and copies ran while one was open for 4% of the time, Pallas kernels for 7%

profile of v2, /device:TPU:0, one launch (start us, length us, event | category | flops | bytes accessed | tf_op | source)
XLA Modules:
  0.0 42.2 jit_solution(11826213751709255946)
XLA Ops:
  0.7 4.1 %collective-permute-start.3 = (bf16[64,576]{1,0:T(8,128)(2,1)}, bf16[64,576]{1,0:T(8,128)(2,1)S(1)}, u32[]{:S(2)}, u32[]{:S(2)}) collective-permute-start(bf16[64,576]{1,0:T(8,128)(2,1)} %refs_0_.1), channel_id=1, source_target_pairs={{0,4},{1,5},{2,6},{3,7},{4,0},{5,1},{6,2},{7,3},{8,12},{9,13},{10,... | collective-permute-start | bytes 221192 | tf_op jit(solution)/shard_map/ppermute | solution.py:236
  4.8 1.6 %collective-permute-start.1 = (bf16[64,576]{1,0:T(8,128)(2,1)}, bf16[64,576]{1,0:T(8,128)(2,1)S(1)}, u32[]{:S(2)}, u32[]{:S(2)}) collective-permute-start(bf16[64,576]{1,0:T(8,128)(2,1)} %refs_0_.1), channel_id=1, source_target_pairs={{0,2},{1,3},{2,0},{3,1},{4,6},{5,7},{6,4},{7,5},{8,10},{9,11},{10,... | collective-permute-start | bytes 221192 | tf_op jit(solution)/shard_map/ppermute | solution.py:236
  6.4 1.5 %collective-permute-start = (bf16[64,576]{1,0:T(8,128)(2,1)}, bf16[64,576]{1,0:T(8,128)(2,1)S(1)}, u32[]{:S(2)}, u32[]{:S(2)}) collective-permute-start(bf16[64,576]{1,0:T(8,128)(2,1)} %refs_0_.1), channel_id=1, source_target_pairs={{0,1},{1,0},{2,3},{3,2},{4,5},{5,4},{6,7},{7,6},{8,9},{9,8},{10,11... | collective-permute-start | bytes 221192 | tf_op jit(solution)/shard_map/ppermute | solution.py:236
  7.9 0.9 %collective-permute-done.3.refs_4_ = bf16[64,576]{1,0:T(8,128)(2,1)S(1)} collective-permute-done((bf16[64,576]{1,0:T(8,128)(2,1)}, bf16[64,576]{1,0:T(8,128)(2,1)S(1)}, u32[]{:S(2)}, u32[]{:S(2)}) %collective-permute-start.3) | collective-permute-done | bytes 73760 | tf_op jit(solution)/shard_map/ppermute | solution.py:236
  8.8 2.2 %collective-permute-start.6 = (bf16[64,576]{1,0:T(8,128)(2,1)S(1)}, bf16[64,576]{1,0:T(8,128)(2,1)S(1)}, u32[]{:S(2)}, u32[]{:S(2)}) collective-permute-start(bf16[64,576]{1,0:T(8,128)(2,1)S(1)} %collective-permute-done.3.refs_4_), channel_id=1, source_target_pairs={{0,3},{1,2},{2,1},{3,0},{4,7},{5,6},{6,5},{7,4},{8,11},{9,10},{10,... | collective-permute-start | bytes 221192 | tf_op jit(solution)/shard_map/ppermute | solution.py:236
  11.0 1.1 %collective-permute-start.5 = (bf16[64,576]{1,0:T(8,128)(2,1)S(1)}, bf16[64,576]{1,0:T(8,128)(2,1)S(1)}, u32[]{:S(2)}, u32[]{:S(2)}) collective-permute-start(bf16[64,576]{1,0:T(8,128)(2,1)S(1)} %collective-permute-done.3.refs_4_), channel_id=1, source_target_pairs={{0,2},{1,3},{2,0},{3,1},{4,6},{5,7},{6,4},{7,5},{8,10},{9,11},{10,... | collective-permute-start | bytes 221192 | tf_op jit(solution)/shard_map/ppermute | solution.py:236
  12.1 0.2 collective-permute-start.4
  12.2 1.9 %collective-permute-start.2 = (bf16[64,576]{1,0:T(8,128)(2,1)S(1)}, bf16[64,576]{1,0:T(8,128)(2,1)S(1)}, u32[]{:S(2)}, u32[]{:S(2)}) collective-permute-start(bf16[64,576]{1,0:T(8,128)(2,1)S(1)} %collective-permute-done.1.refs_2_), channel_id=1, source_target_pairs={{0,1},{1,0},{2,3},{3,2},{4,5},{5,4},{6,7},{7,6},{8,9},{9,8},{10,11... | collective-permute-start | bytes 221192 | tf_op jit(solution)/shard_map/ppermute | solution.py:236
  14.1 0.9 %pad_maximum_fusion = bf16[256,576]{1,0:T(8,128)(2,1)S(1)} fusion(bf16[64,576]{1,0:T(8,128)(2,1)S(1)} %collective-permute-done.refs_1_, bf16[64,576]{1,0:T(8,128)(2,1)S(1)} %collective-permute-done.3.refs_4_, bf16[64,576]{1,0:T(8,128)(2,1)S(1)} %collective-permute-done.1.refs_2_, bf16[64,576]{1,0:T(8,128)(2,1)} %refs_0_.1), kind=kLoop, calls=%fused_computation | loop fusion | flops 1179648 | bytes 589824 | tf_op jit(solution)/shard_map/concatenate | solution.py:266
  15.1 0.5 %collective-permute-done.5.refs_6_ = bf16[64,576]{1,0:T(8,128)(2,1)S(1)} collective-permute-done((bf16[64,576]{1,0:T(8,128)(2,1)S(1)}, bf16[64,576]{1,0:T(8,128)(2,1)S(1)}, u32[]{:S(2)}, u32[]{:S(2)}) %collective-permute-start.5) | collective-permute-done | bytes 73760 | tf_op jit(solution)/shard_map/ppermute | solution.py:236
  15.6 0.9 %collective-permute-done.4.refs_5_ = bf16[64,576]{1,0:T(8,128)(2,1)S(1)} collective-permute-done((bf16[64,576]{1,0:T(8,128)(2,1)S(1)}, bf16[64,576]{1,0:T(8,128)(2,1)S(1)}, u32[]{:S(2)}, u32[]{:S(2)}) %collective-permute-start.4) | collective-permute-done | bytes 73760 | tf_op jit(solution)/shard_map/ppermute | solution.py:236
  16.5 0.9 %collective-permute-done.2.refs_3_ = bf16[64,576]{1,0:T(8,128)(2,1)S(1)} collective-permute-done((bf16[64,576]{1,0:T(8,128)(2,1)S(1)}, bf16[64,576]{1,0:T(8,128)(2,1)S(1)}, u32[]{:S(2)}, u32[]{:S(2)}) %collective-permute-start.2) | collective-permute-done | bytes 73760 | tf_op jit(solution)/shard_map/ppermute | solution.py:236
  17.6 1.3 %shard_map.59 = (bf16[512,576]{1,0:T(8,128)(2,1)S(1)}, f32[512,512]{1,0:T(8,128)S(1)}, f32[512,512]{1,0:T(8,128)S(1)}, f32[1,512]{1,0:T(1,128)S(1)}) custom-call(s32[2]{0:T(128)S(1)} %pad_add_fusion.scalars, bf16[576,512]{1,0:T(8,128)(2,1)S(1)} %bitcast.11, bf16[512,512]{1,0:T(8,128)(2,1)S(1)} %bitcast.14, bf16[64,576]{1,0:T(8,128)(2,1)S(1)} %copy-done.2, ...), custom_call_target="tpu_custom_call" | custom-call | tf_op jit(solution)/shard_map/pallas_call | solution.py:218
  18.9 0.2 collective-permute-done.8.refs_1_
  19.1 1.1 %shard_map.60 = (bf16[512,576]{1,0:T(8,128)(2,1)S(1)}, bf16[512,640]{1,0:T(8,128)(2,1)S(1)}, bf16[512,512]{1,0:T(8,128)(2,1)S(1)}, bf16[512,512]{1,0:T(8,128)(2,1)S(1)}, bf16[512,512]{1,0:T(8,128)(2,1)S(1)}) custom-call(s32[2]{0:T(128)S(1)} %pad_add_fusion.scalars, s32[1,512]{1,0:T(1,128)S(1)} %bitcast.17, bf16[576,512]{1,0:T(8,128)(2,1)S(1)} %bitcast.12, ...), custom_call_target="tpu_custom_call" | custom-call | tf_op jit(solution)/shard_map/pallas_call | solution.py:218
  20.3 2.7 %collective-permute-start.9 = (bf16[512,640]{1,0:T(8,128)(2,1)S(1)}, bf16[512,640]{1,0:T(8,128)(2,1)S(1)}, u32[]{:S(2)}, u32[]{:S(2)}) collective-permute-start(bf16[512,640]{1,0:T(8,128)(2,1)S(1)} %get-tuple-element.27), channel_id=1, source_target_pairs={{0,8},{8,0},{1,9},{9,1},{2,10},{10,2},{3,11},{11,3},{4,12},{12,4},... | collective-permute-start | bytes 1966088 | tf_op jit(solution)/shard_map/ppermute | solution.py:231
  23.0 0.7 %shard_map.62.own_ref = f32[512,640]{1,0:T(8,128)S(1)} custom-call(bf16[576,512]{1,0:T(8,128)(2,1)S(1)} %bitcast.13, bf16[512,512]{1,0:T(8,128)(2,1)S(1)} %bitcast.16, bf16[512,512]{1,0:T(8,128)(2,1)S(1)} %get-tuple-element.25.own_sg_ref, bf16[512,512]{1,0:T(8,128)(2,1)S(1)} %get-tuple-element.26.own_probs_ref), custom_call_target="tpu_custom_call" | custom-call | tf_op jit(solution)/shard_map/pallas_call | solution.py:218
  23.7 1.0 %collective-permute-done.9.later_ref = bf16[512,640]{1,0:T(8,128)(2,1)S(1)} collective-permute-done((bf16[512,640]{1,0:T(8,128)(2,1)S(1)}, bf16[512,640]{1,0:T(8,128)(2,1)S(1)}, u32[]{:S(2)}, u32[]{:S(2)}) %collective-permute-start.9) | collective-permute-done | bytes 655392 | tf_op jit(solution)/shard_map/ppermute | solution.py:231
  24.7 0.7 %shard_map.63 = (f32[64,640]{1,0:T(8,128)S(1)}, bf16[64,640]{1,0:T(8,128)(2,1)S(1)}, f32[64,640]{1,0:T(8,128)S(1)}, bf16[64,640]{1,0:T(8,128)(2,1)S(1)}, f32[64,...) custom-call(s32[2]{0:T(128)S(1)} %pad_add_fusion.scalars, ...), custom_call_target="tpu_custom_call" | custom-call | tf_op jit(solution)/shard_map/pallas_call | solution.py:218
  25.4 1.2 %collective-permute-start.10 = (bf16[64,640]{1,0:T(8,128)(2,1)S(1)}, bf16[64,640]{1,0:T(8,128)(2,1)S(1)}, u32[]{:S(2)}, u32[]{:S(2)}) collective-permute-start(bf16[64,640]{1,0:T(8,128)(2,1)S(1)} %get-tuple-element.30), channel_id=1, source_target_pairs={{0,1},{1,0},{2,3},{3,2},{4,5},{5,4},{6,7},{7,6},{8,9},{9,8},{10,11... | collective-permute-start | bytes 245768 | tf_op jit(solution)/shard_map/ppermute | solution.py:236
  26.6 1.9 %collective-permute-start.12 = (bf16[64,640]{1,0:T(8,128)(2,1)S(1)}, bf16[64,640]{1,0:T(8,128)(2,1)S(1)}, u32[]{:S(2)}, u32[]{:S(2)}) collective-permute-start(bf16[64,640]{1,0:T(8,128)(2,1)S(1)} %get-tuple-element.32), channel_id=1, source_target_pairs={{0,3},{1,2},{2,1},{3,0},{4,7},{5,6},{6,5},{7,4},{8,11},{9,10},{10,... | collective-permute-start | bytes 245768 | tf_op jit(solution)/shard_map/ppermute | solution.py:236
  28.5 1.0 %collective-permute-start.13 = (bf16[64,640]{1,0:T(8,128)(2,1)S(1)}, bf16[64,640]{1,0:T(8,128)(2,1)S(1)}, u32[]{:S(2)}, u32[]{:S(2)}) collective-permute-start(bf16[64,640]{1,0:T(8,128)(2,1)S(1)} %get-tuple-element.33), channel_id=1, source_target_pairs={{0,1},{1,0},{2,3},{3,2},{4,5},{5,4},{6,7},{7,6},{8,9},{9,8},{10,11... | collective-permute-start | bytes 245768 | tf_op jit(solution)/shard_map/ppermute | solution.py:236
  29.5 0.6 %collective-permute-start.14 = (bf16[64,640]{1,0:T(8,128)(2,1)S(1)}, bf16[64,640]{1,0:T(8,128)(2,1)S(1)}, u32[]{:S(2)}, u32[]{:S(2)}) collective-permute-start(bf16[64,640]{1,0:T(8,128)(2,1)S(1)} %get-tuple-element.34), channel_id=1, source_target_pairs={{0,2},{1,3},{2,0},{3,1},{4,6},{5,7},{6,4},{7,5},{8,10},{9,11},{10,... | collective-permute-start | bytes 245768 | tf_op jit(solution)/shard_map/ppermute | solution.py:236
  30.1 0.9 %collective-permute-start.16 = (bf16[64,640]{1,0:T(8,128)(2,1)S(1)}, bf16[64,640]{1,0:T(8,128)(2,1)S(1)}, u32[]{:S(2)}, u32[]{:S(2)}) collective-permute-start(bf16[64,640]{1,0:T(8,128)(2,1)S(1)} %get-tuple-element.35), channel_id=1, source_target_pairs={{0,1},{1,0},{2,3},{3,2},{4,5},{5,4},{6,7},{7,6},{8,9},{9,8},{10,11... | collective-permute-start | bytes 245768 | tf_op jit(solution)/shard_map/ppermute | solution.py:236
  31.0 2.6 %collective-permute-start.11 = (bf16[64,640]{1,0:T(8,128)(2,1)S(1)}, bf16[64,640]{1,0:T(8,128)(2,1)S(1)}, u32[]{:S(2)}, u32[]{:S(2)}) collective-permute-start(bf16[64,640]{1,0:T(8,128)(2,1)S(1)} %shard_map.64), channel_id=1, source_target_pairs={{0,2},{1,3},{2,0},{3,1},{4,6},{5,7},{6,4},{7,5},{8,10},{9,11},{10,... | collective-permute-start | bytes 245768 | tf_op jit(solution)/shard_map/ppermute | solution.py:236
  33.6 0.2 collective-permute-done.13.refs_2_
  33.8 0.5 %collective-permute-done.14.refs_3_ = bf16[64,640]{1,0:T(8,128)(2,1)S(1)} collective-permute-done((bf16[64,640]{1,0:T(8,128)(2,1)S(1)}, bf16[64,640]{1,0:T(8,128)(2,1)S(1)}, u32[]{:S(2)}, u32[]{:S(2)}) %collective-permute-start.14) | collective-permute-done | bytes 81952 | tf_op jit(solution)/shard_map/ppermute | solution.py:236
  34.4 3.4 %collective-permute-start.15 = (bf16[64,640]{1,0:T(8,128)(2,1)S(1)}, bf16[64,640]{1,0:T(8,128)(2,1)S(1)}, u32[]{:S(2)}, u32[]{:S(2)}) collective-permute-start(bf16[64,640]{1,0:T(8,128)(2,1)S(1)} %shard_map.65), channel_id=1, source_target_pairs={{0,4},{1,5},{2,6},{3,7},{4,0},{5,1},{6,2},{7,3},{8,12},{9,13},{10,... | collective-permute-start | bytes 245768 | tf_op jit(solution)/shard_map/ppermute | solution.py:236
  37.7 1.0 %shard_map.61 = bf16[576,512]{1,0:T(8,128)(2,1)S(1)} custom-call(s32[2]{0:T(128)S(1)} %pad_add_fusion.scalars, bf16[512,576]{1,0:T(8,128)(2,1)S(1)} %get-tuple-element.22.prev_keys_ref, bf16[512,576]{1,0:T(8,128)(2,1)S(1)} %get-tuple-element.23.own_keys_ref, bf16[512,512]{1,0:T(8,128)(2,1)S(1)} %get-tuple-element.24.prev_sg_ref, ...), custom_call_target="tpu_custom_call" | custom-call | tf_op jit(solution)/shard_map/pallas_call | solution.py:218
  38.8 0.8 %copy.6 = bf16[512,1,576]{0,2,1:T(8,128)(2,1)} copy(bf16[512,1,576]{0,2,1:T(8,128)(2,1)S(1)} %bitcast.10) | data formatting | bytes 1179648
  39.6 1.9 %collective-permute-done.15.refs_2_ = bf16[64,640]{1,0:T(8,128)(2,1)S(1)} collective-permute-done((bf16[64,640]{1,0:T(8,128)(2,1)S(1)}, bf16[64,640]{1,0:T(8,128)(2,1)S(1)}, u32[]{:S(2)}, u32[]{:S(2)}) %collective-permute-start.15) | collective-permute-done | bytes 81952 | tf_op jit(solution)/shard_map/ppermute | solution.py:236
  41.6 0.6 %copy.7 = bf16[64,576]{1,0:T(8,128)(2,1)} copy(bf16[64,576]{1,0:T(8,128)(2,1)S(1)} %shard_map.66) | data formatting | bytes 147456
  (23 shorter events, 0.4 us)
Async XLA Ops:
  0.6 17.0 %copy-start.2 = (bf16[64,576]{1,0:T(8,128)(2,1)S(1)}, bf16[64,576]{1,0:T(8,128)(2,1)}, u32[]{:S(2)}) copy-start(bf16[64,576]{1,0:T(8,128)(2,1)} %refs_0_.1) | copy-start | bytes 221188
  0.6 17.0 %copy-start.1 = (bf16[512,1,512]{2,0,1:T(8,128)(2,1)S(1)}, bf16[512,1,512]{2,0,1:T(8,128)(2,1)}, u32[]{:S(2)}) copy-start(bf16[512,1,512]{2,0,1:T(8,128)(2,1)} %param.6) | copy-start | bytes 1572868
  0.6 17.0 %copy-start = (bf16[512,1,576]{0,2,1:T(8,128)(2,1)S(1)}, bf16[512,1,576]{0,2,1:T(8,128)(2,1)}, u32[]{:S(2)}) copy-start(bf16[512,1,576]{0,2,1:T(8,128)(2,1)} %param.4) | copy-start | bytes 1769476
  0.7 8.1 %collective-permute-start.3 = (bf16[64,576]{1,0:T(8,128)(2,1)}, bf16[64,576]{1,0:T(8,128)(2,1)S(1)}, u32[]{:S(2)}, u32[]{:S(2)}) collective-permute-start(bf16[64,576]{1,0:T(8,128)(2,1)} %refs_0_.1), channel_id=1, source_target_pairs={{0,4},{1,5},{2,6},{3,7},{4,0},{5,1},{6,2},{7,3},{8,12},{9,13},{10,... | collective-permute-start | bytes 221192 | tf_op jit(solution)/shard_map/ppermute | solution.py:236
  4.8 7.5 %collective-permute-start.1 = (bf16[64,576]{1,0:T(8,128)(2,1)}, bf16[64,576]{1,0:T(8,128)(2,1)S(1)}, u32[]{:S(2)}, u32[]{:S(2)}) collective-permute-start(bf16[64,576]{1,0:T(8,128)(2,1)} %refs_0_.1), channel_id=1, source_target_pairs={{0,2},{1,3},{2,0},{3,1},{4,6},{5,7},{6,4},{7,5},{8,10},{9,11},{10,... | collective-permute-start | bytes 221192 | tf_op jit(solution)/shard_map/ppermute | solution.py:236
  6.4 7.8 %collective-permute-start = (bf16[64,576]{1,0:T(8,128)(2,1)}, bf16[64,576]{1,0:T(8,128)(2,1)S(1)}, u32[]{:S(2)}, u32[]{:S(2)}) collective-permute-start(bf16[64,576]{1,0:T(8,128)(2,1)} %refs_0_.1), channel_id=1, source_target_pairs={{0,1},{1,0},{2,3},{3,2},{4,5},{5,4},{6,7},{7,6},{8,9},{9,8},{10,11... | collective-permute-start | bytes 221192 | tf_op jit(solution)/shard_map/ppermute | solution.py:236
  8.8 6.4 %collective-permute-start.6 = (bf16[64,576]{1,0:T(8,128)(2,1)S(1)}, bf16[64,576]{1,0:T(8,128)(2,1)S(1)}, u32[]{:S(2)}, u32[]{:S(2)}) collective-permute-start(bf16[64,576]{1,0:T(8,128)(2,1)S(1)} %collective-permute-done.3.refs_4_), channel_id=1, source_target_pairs={{0,3},{1,2},{2,1},{3,0},{4,7},{5,6},{6,5},{7,4},{8,11},{9,10},{10,... | collective-permute-start | bytes 221192 | tf_op jit(solution)/shard_map/ppermute | solution.py:236
  11.0 4.7 %collective-permute-start.5 = (bf16[64,576]{1,0:T(8,128)(2,1)S(1)}, bf16[64,576]{1,0:T(8,128)(2,1)S(1)}, u32[]{:S(2)}, u32[]{:S(2)}) collective-permute-start(bf16[64,576]{1,0:T(8,128)(2,1)S(1)} %collective-permute-done.3.refs_4_), channel_id=1, source_target_pairs={{0,2},{1,3},{2,0},{3,1},{4,6},{5,7},{6,4},{7,5},{8,10},{9,11},{10,... | collective-permute-start | bytes 221192 | tf_op jit(solution)/shard_map/ppermute | solution.py:236
  12.1 4.4 %collective-permute-start.4 = (bf16[64,576]{1,0:T(8,128)(2,1)S(1)}, bf16[64,576]{1,0:T(8,128)(2,1)S(1)}, u32[]{:S(2)}, u32[]{:S(2)}) collective-permute-start(bf16[64,576]{1,0:T(8,128)(2,1)S(1)} %collective-permute-done.3.refs_4_), channel_id=1, source_target_pairs={{0,1},{1,0},{2,3},{3,2},{4,5},{5,4},{6,7},{7,6},{8,9},{9,8},{10,11... | collective-permute-start | bytes 221192 | tf_op jit(solution)/shard_map/ppermute | solution.py:236
  12.2 5.2 %collective-permute-start.2 = (bf16[64,576]{1,0:T(8,128)(2,1)S(1)}, bf16[64,576]{1,0:T(8,128)(2,1)S(1)}, u32[]{:S(2)}, u32[]{:S(2)}) collective-permute-start(bf16[64,576]{1,0:T(8,128)(2,1)S(1)} %collective-permute-done.1.refs_2_), channel_id=1, source_target_pairs={{0,1},{1,0},{2,3},{3,2},{4,5},{5,4},{6,7},{7,6},{8,9},{9,8},{10,11... | collective-permute-start | bytes 221192 | tf_op jit(solution)/shard_map/ppermute | solution.py:236
  15.0 4.1 %copy-start.3 = (s32[512]{0:T(512)S(1)}, s32[512]{0:T(512)}, u32[]{:S(2)}) copy-start(s32[512]{0:T(512)} %param.7) | copy-start | bytes 6148
  15.1 3.8 %collective-permute-start.7 = (bf16[256,576]{1,0:T(8,128)(2,1)S(1)}, bf16[256,576]{1,0:T(8,128)(2,1)S(1)}, u32[]{:S(2)}, u32[]{:S(2)}) collective-permute-start(bf16[256,576]{1,0:T(8,128)(2,1)S(1)} %pad_maximum_fusion), channel_id=1, source_target_pairs={{0,8},{8,0},{1,9},{9,1},{2,10},{10,2},{3,11},{11,3},{4,12},{12,4},... | collective-permute-start | bytes 884744 | tf_op jit(solution)/shard_map/ppermute | solution.py:231
  17.4 1.7 %collective-permute-start.8 = (bf16[256,576]{1,0:T(8,128)(2,1)S(1)}, bf16[256,576]{1,0:T(8,128)(2,1)S(1)}, u32[]{:S(2)}, u32[]{:S(2)}) collective-permute-start(bf16[256,576]{1,0:T(8,128)(2,1)S(1)} %pad_maximum_fusion.1), channel_id=1, source_target_pairs={{0,8},{8,0},{1,9},{9,1},{2,10},{10,2},{3,11},{11,3},{4,12},{12,4},... | collective-permute-start | bytes 884744 | tf_op jit(solution)/shard_map/ppermute | solution.py:231
  20.3 4.4 %collective-permute-start.9 = (bf16[512,640]{1,0:T(8,128)(2,1)S(1)}, bf16[512,640]{1,0:T(8,128)(2,1)S(1)}, u32[]{:S(2)}, u32[]{:S(2)}) collective-permute-start(bf16[512,640]{1,0:T(8,128)(2,1)S(1)} %get-tuple-element.27), channel_id=1, source_target_pairs={{0,8},{8,0},{1,9},{9,1},{2,10},{10,2},{3,11},{11,3},{4,12},{12,4},... | collective-permute-start | bytes 1966088 | tf_op jit(solution)/shard_map/ppermute | solution.py:231
  25.4 5.6 %collective-permute-start.10 = (bf16[64,640]{1,0:T(8,128)(2,1)S(1)}, bf16[64,640]{1,0:T(8,128)(2,1)S(1)}, u32[]{:S(2)}, u32[]{:S(2)}) collective-permute-start(bf16[64,640]{1,0:T(8,128)(2,1)S(1)} %get-tuple-element.30), channel_id=1, source_target_pairs={{0,1},{1,0},{2,3},{3,2},{4,5},{5,4},{6,7},{7,6},{8,9},{9,8},{10,11... | collective-permute-start | bytes 245768 | tf_op jit(solution)/shard_map/ppermute | solution.py:236
  26.6 7.0 %collective-permute-start.12 = (bf16[64,640]{1,0:T(8,128)(2,1)S(1)}, bf16[64,640]{1,0:T(8,128)(2,1)S(1)}, u32[]{:S(2)}, u32[]{:S(2)}) collective-permute-start(bf16[64,640]{1,0:T(8,128)(2,1)S(1)} %get-tuple-element.32), channel_id=1, source_target_pairs={{0,3},{1,2},{2,1},{3,0},{4,7},{5,6},{6,5},{7,4},{8,11},{9,10},{10,... | collective-permute-start | bytes 245768 | tf_op jit(solution)/shard_map/ppermute | solution.py:236
  28.5 5.3 %collective-permute-start.13 = (bf16[64,640]{1,0:T(8,128)(2,1)S(1)}, bf16[64,640]{1,0:T(8,128)(2,1)S(1)}, u32[]{:S(2)}, u32[]{:S(2)}) collective-permute-start(bf16[64,640]{1,0:T(8,128)(2,1)S(1)} %get-tuple-element.33), channel_id=1, source_target_pairs={{0,1},{1,0},{2,3},{3,2},{4,5},{5,4},{6,7},{7,6},{8,9},{9,8},{10,11... | collective-permute-start | bytes 245768 | tf_op jit(solution)/shard_map/ppermute | solution.py:236
  29.5 4.8 %collective-permute-start.14 = (bf16[64,640]{1,0:T(8,128)(2,1)S(1)}, bf16[64,640]{1,0:T(8,128)(2,1)S(1)}, u32[]{:S(2)}, u32[]{:S(2)}) collective-permute-start(bf16[64,640]{1,0:T(8,128)(2,1)S(1)} %get-tuple-element.34), channel_id=1, source_target_pairs={{0,2},{1,3},{2,0},{3,1},{4,6},{5,7},{6,4},{7,5},{8,10},{9,11},{10,... | collective-permute-start | bytes 245768 | tf_op jit(solution)/shard_map/ppermute | solution.py:236
  30.1 9.5 %collective-permute-start.16 = (bf16[64,640]{1,0:T(8,128)(2,1)S(1)}, bf16[64,640]{1,0:T(8,128)(2,1)S(1)}, u32[]{:S(2)}, u32[]{:S(2)}) collective-permute-start(bf16[64,640]{1,0:T(8,128)(2,1)S(1)} %get-tuple-element.35), channel_id=1, source_target_pairs={{0,1},{1,0},{2,3},{3,2},{4,5},{5,4},{6,7},{7,6},{8,9},{9,8},{10,11... | collective-permute-start | bytes 245768 | tf_op jit(solution)/shard_map/ppermute | solution.py:236
  31.0 8.6 %collective-permute-start.11 = (bf16[64,640]{1,0:T(8,128)(2,1)S(1)}, bf16[64,640]{1,0:T(8,128)(2,1)S(1)}, u32[]{:S(2)}, u32[]{:S(2)}) collective-permute-start(bf16[64,640]{1,0:T(8,128)(2,1)S(1)} %shard_map.64), channel_id=1, source_target_pairs={{0,2},{1,3},{2,0},{3,1},{4,6},{5,7},{6,4},{7,5},{8,10},{9,11},{10,... | collective-permute-start | bytes 245768 | tf_op jit(solution)/shard_map/ppermute | solution.py:236
  34.4 7.1 %collective-permute-start.15 = (bf16[64,640]{1,0:T(8,128)(2,1)S(1)}, bf16[64,640]{1,0:T(8,128)(2,1)S(1)}, u32[]{:S(2)}, u32[]{:S(2)}) collective-permute-start(bf16[64,640]{1,0:T(8,128)(2,1)S(1)} %shard_map.65), channel_id=1, source_target_pairs={{0,4},{1,5},{2,6},{3,7},{4,0},{5,1},{6,2},{7,3},{8,12},{9,13},{10,... | collective-permute-start | bytes 245768 | tf_op jit(solution)/shard_map/ppermute | solution.py:236
